TPU v7x, 32 devices: a whole 2x2x4 slice. The times are simulated.
32 devices in a mesh: expert: 16 (over z, y, x), pair: 2 (over core).
Axes of the slice: x: 2, y: 2, z: 4, core: 2. Of those that a mesh axis runs over, the one named last changes fastest.
Arguments:
- tokens: bfloat16 [192, 196, 1024], P(('expert', 'pair')), may hold values from -64 to 64
- router: bfloat16 [1024, 16], replicated, as said below
- w_in: bfloat16 [16, 1024, 4096], P('expert', None, 'pair'), may hold values from -0.1875 to 0.1875
- w_out: bfloat16 [16, 4096, 1024], P('expert', 'pair'), may hold values from -0.09375 to 0.09375
- out_grad: bfloat16 [192, 196, 1024], P(('expert', 'pair')), may hold values from -6 to 6
Outputs:
- tokens_grad: bfloat16 [192, 196, 1024], P(('expert', 'pair'))
- w_in_grad: bfloat16 [16, 1024, 4096], P('expert', None, 'pair')
- w_out_grad: bfloat16 [16, 4096, 1024], P('expert', 'pair')
- router_grad: float32 [1024, 16], replicated
Inputs may be any that keep to these rules, and one draw needn't show every extreme that they name: `router`: entries are normal with deviation 1024 ** -0.5, cut at five deviations.
All inputs are finite; a program needn't handle non-finite values.
Results may differ from a plain program's by a relative error of at most 0.0087.
Values may be sent and summed in bfloat16 or wider, within the bound.
No kernel may reach another device: no remote copies, remote signals or barrier semaphores. Data moves between devices by JAX's collectives and lax.ppermute only.
A program may use at most 128 MiB of HBM per device.

v0:
```python
import functools
import math

import jax
import jax.numpy as jnp
from jax import lax
from jax.experimental import pallas as pl
from jax.experimental.pallas import tpu as pltpu
from jax.sharding import PartitionSpec as P


BF = jnp.bfloat16
F32 = jnp.float32
ROOT = math.sqrt(2.0 / math.pi)
CUBE = 0.044715
VM = pl.BlockSpec(memory_space=pltpu.VMEM)
HBM = pl.BlockSpec(memory_space=pltpu.HBM)


def in_hbm(x):
    return pltpu.with_memory_space_constraint(x, pltpu.HBM)


def mm(a, b, da=1, db=0):
    return lax.dot_general(a, b, (((da,), (db,)), ((), ())), preferred_element_type=F32)


def params(mib, **more):
    return pltpu.CompilerParams(vmem_limit_bytes=mib << 20, **more)


def cost(flops, nbytes):
    return pl.CostEstimate(flops=flops, bytes_accessed=nbytes, transcendentals=0)


def pieces_of(local_count):
    return 8 // math.gcd(2 * local_count, 8)


def spread(kind, count, pieces, experts):
    block = pieces * kind
    expert = lax.broadcasted_iota(jnp.int32, (experts, block, kind * experts), 0)
    place = lax.broadcasted_iota(jnp.int32, (experts, block, kind * experts), 1)
    source = lax.broadcasted_iota(jnp.int32, (experts, block, kind * experts), 2)
    hit = source == (place - count * kind) * experts + expert
    hit = hit & (place >= count * kind) & (place < (count + 1) * kind)
    return jnp.where(hit, 1.0, 0.0).astype(BF).reshape(experts * block, kind * experts)


def gather(kind, count, pieces, experts, minor):
    block = pieces * kind
    column = lax.broadcasted_iota(jnp.int32, (1, experts * block), 1)
    expert = column // block
    place = column - expert * block - count * kind
    wanted = minor(place, expert)
    wanted = jnp.where((place >= 0) & (place < kind), wanted, -1)
    row = lax.broadcasted_iota(jnp.int32, (kind * experts, experts * block), 0)
    return jnp.where(row == wanted, 1.0, 0.0).astype(BF)


def slots_kernel(
    pieces, tok_hbm, cot_hbm, router_hbm, first, second,
    send, disp, comb, router, held_first, held_second,
    tok, cot, rows, sems, more_sems,
):
    images, _, width = tok_hbm.shape
    experts = router.shape[0]
    router_copy = pltpu.make_async_copy(router_hbm, router, more_sems.at[0])
    router_copy.start()
    held = (
        pltpu.make_async_copy(first, held_first, more_sems.at[1]),
        pltpu.make_async_copy(second, held_second, more_sems.at[2]),
    )
    part = width // pieces
    copies = []
    for n in range(images):
        pair = (
            pltpu.make_async_copy(tok_hbm.at[n], tok.at[n], sems.at[0, n]),
            pltpu.make_async_copy(cot_hbm.at[n], cot.at[n], sems.at[1, n]),
        )
        pair[0].start()
        pair[1].start()
        copies.append(pair)
    for copy in held:
        copy.start()
    router_copy.wait()
    for n in range(images):
        copies[n][0].wait()
        logits = mm(router[...], tok[n], 1, 1)
        top = jnp.exp(logits - jnp.max(logits, axis=1, keepdims=True))
        dispatch = top / jnp.sum(top, axis=1, keepdims=True)
        top = jnp.exp(logits - jnp.max(logits, axis=0, keepdims=True))
        combine = top / jnp.sum(top, axis=0, keepdims=True)
        disp[n] = dispatch
        comb[n] = combine
        rows[pl.ds(n * experts, experts), :] = mm(dispatch.astype(BF), tok[n]).astype(BF)
        copies[n][1].wait()
        rows[pl.ds((images + n) * experts, experts), :] = mm(combine.astype(BF), cot[n]).astype(BF)
    kind = 2 * images
    total = None
    for count in range(pieces):
        term = mm(spread(kind, count, pieces, experts), rows[:, count * part : (count + 1) * part])
        total = term if total is None else total + term
    send[...] = total.astype(BF)
    for copy in held:
        copy.wait()


def make_slots(tokens, out_grad, router_t, first, second):
    images, toks, width = tokens.shape
    experts = router_t.shape[0]
    pieces = pieces_of(images)
    block = 2 * images * pieces
    return pl.pallas_call(
        functools.partial(slots_kernel, pieces),
        out_shape=(
            jax.ShapeDtypeStruct((experts * block, width // pieces), BF),
            pltpu.VMEM((images, experts, toks), F32),
            pltpu.VMEM((images, experts, toks), F32),
            pltpu.VMEM(router_t.shape, BF),
            pltpu.VMEM(first.shape, BF),
            pltpu.VMEM(second.shape, BF),
        ),
        in_specs=[HBM] * 5,
        out_specs=(VM,) * 6,
        scratch_shapes=[
            pltpu.VMEM(tokens.shape, BF),
            pltpu.VMEM(tokens.shape, BF),
            pltpu.VMEM((2 * images * experts, width), BF),
            pltpu.SemaphoreType.DMA((2, images)),
            pltpu.SemaphoreType.DMA((3,)),
        ],
        compiler_params=params(16),
        cost_estimate=cost(6 * images * toks * width * experts, 4 * images * toks * width),
        name="slots",
    )(*(in_hbm(x) for x in (tokens, out_grad, router_t, first, second)))


def expert_kernel(
    pieces, images, mine, theirs, w_in, w_out, keep, give, slot, cot, act, hgrad
):
    half = mine.shape[0] // (2 * pieces)
    part = mine.shape[1]
    width = pieces * part
    hidden = w_in.shape[1]
    kind = 2 * images
    groups = mine.shape[0] // (pieces * kind)
    for count in range(pieces):
        pick = gather(
            kind,
            count,
            pieces,
            groups,
            lambda place, source: jnp.where(
                place >= images,
                groups * images + source * images + place - images,
                source * images + place,
            ),
        )
        columns = slice(count * part, (count + 1) * part)
        for base, ref in ((0, mine), (half, theirs)):
            both = mm(pick, ref[...]).astype(BF)
            slot[base : base + half, columns] = both[:half]
            cot[base : base + half, columns] = both[half:]
    step = 256
    for f in range(0, hidden, step):
        x = mm(slot[...], w_in[:, f : f + step])
        g = mm(cot[...], w_out[f : f + step, :], 1, 1)
        square = x * x
        t = jnp.tanh(ROOT * x * (1.0 + CUBE * square))
        up = 0.5 + 0.5 * t
        act[:, f : f + step] = (x * up).astype(BF)
        slope = up + x * (0.5 * ROOT) * (1.0 - t * t) * (1.0 + (3.0 * CUBE) * square)
        hgrad[:, f : f + step] = (g * slope).astype(BF)
    step = 256
    for c in range(0, width, step):
        columns = slice(c, c + step)
        value = mm(act[...], w_out[:, columns])
        keep[:half, columns] = value[:half]
        give[:half, columns] = value[half:].astype(BF)
        value = mm(hgrad[...], w_in[columns, :], 1, 1)
        keep[half:, columns] = value[:half]
        give[half:, columns] = value[half:].astype(BF)


def run_expert(mine, theirs, w_in, w_out, images):
    pieces = pieces_of(images)
    rows = mine.shape[0] // pieces
    width = w_in.shape[0]
    hidden = w_in.shape[1]
    return pl.pallas_call(
        functools.partial(expert_kernel, pieces, images),
        out_shape=(
            jax.ShapeDtypeStruct((rows, width), F32),
            jax.ShapeDtypeStruct((rows, width), BF),
            jax.ShapeDtypeStruct((rows, width), BF),
            jax.ShapeDtypeStruct((rows, width), BF),
            jax.ShapeDtypeStruct((rows, hidden), BF),
            jax.ShapeDtypeStruct((rows, hidden), BF),
        ),
        in_specs=[VM] * 4,
        out_specs=(VM,) * 6,
        compiler_params=params(32),
        cost_estimate=cost(8 * rows * width * hidden, 4 * width * hidden),
        name="expert",
    )(mine, theirs, w_in, w_out)


def join_kernel(pieces, images, keep, got, send):
    kind = 2 * images
    part = send.shape[1]
    groups = send.shape[0] // (pieces * kind)
    both = (keep[...] + got[...].astype(F32)).astype(BF)
    total = None
    for count in range(pieces):
        pick = join_pick(kind, images, count, pieces, groups)
        term = mm(pick, both[:, count * part : (count + 1) * part])
        total = term if total is None else total + term
    send[...] = total.astype(BF)


def join_pick(kind, images, count, pieces, groups):
    block = pieces * kind
    shape = (groups, block, kind * groups)
    group = lax.broadcasted_iota(jnp.int32, shape, 0)
    place = lax.broadcasted_iota(jnp.int32, shape, 1) - count * kind
    source = lax.broadcasted_iota(jnp.int32, shape, 2)
    wanted = jnp.where(
        place >= images, groups * images + group * images + place - images, group * images + place
    )
    hit = (source == wanted) & (place >= 0) & (place < kind)
    return jnp.where(hit, 1.0, 0.0).astype(BF).reshape(groups * block, kind * groups)


def join(keep, got, images):
    pieces = pieces_of(images)
    rows, width = keep.shape
    return pl.pallas_call(
        functools.partial(join_kernel, pieces, images),
        out_shape=jax.ShapeDtypeStruct((rows * pieces, width // pieces), BF),
        in_specs=[VM] * 2,
        out_specs=VM,
        compiler_params=params(8),
        cost_estimate=cost(4 * rows * rows * width, 8 * rows * width),
        name="join",
    )(keep, got)


def logits_kernel(
    pieces, back, tok_hbm, cot_hbm, disp, comb, part_out, lgrad, sgrad, tok, cot, rows, sems
):
    images, experts, _ = disp.shape
    copies = []
    for n in range(images):
        pair = (
            pltpu.make_async_copy(cot_hbm.at[n], cot.at[n], sems.at[1, n]),
            pltpu.make_async_copy(tok_hbm.at[n], tok.at[n], sems.at[0, n]),
        )
        pair[0].start()
        pair[1].start()
        copies.append(pair)
    kind = 2 * images
    part = back.shape[1]
    for count in range(pieces):
        pick = gather(
            kind, count, pieces, experts, lambda place, expert: place * experts + expert
        )
        rows[:, count * part : (count + 1) * part] = mm(pick, back[...]).astype(BF)
    total = None
    for n in range(images):
        combine = comb[n]
        dispatch = disp[n]
        copies[n][0].wait()
        copies[n][1].wait()
        slot = rows[(images + n) * experts : (images + n + 1) * experts, :]
        c = mm(rows[n * experts : (n + 1) * experts, :], cot[n], 1, 1)
        d = mm(slot, tok[n], 1, 1)
        c = combine * (c - jnp.sum(combine * c, axis=0, keepdims=True))
        d = dispatch * (d - jnp.sum(dispatch * d, axis=1, keepdims=True))
        both = (c + d).astype(BF)
        lgrad[n] = both
        sgrad[n] = slot
        term = mm(both, tok[n])
        total = term if total is None else total + term
    part_out[...] = total


def logit_grads(back, tok, cot, disp, comb):
    images, experts, toks = disp.shape
    width = tok.shape[2]
    pieces = pieces_of(images)
    return pl.pallas_call(
        functools.partial(logits_kernel, pieces),
        out_shape=(
            jax.ShapeDtypeStruct((experts, width), F32),
            jax.ShapeDtypeStruct((images, experts, toks), BF),
            jax.ShapeDtypeStruct((images, experts, width), BF),
        ),
        in_specs=[VM, HBM, HBM, VM, VM],
        out_specs=(VM,) * 3,
        scratch_shapes=[
            pltpu.VMEM(tok.shape, BF),
            pltpu.VMEM(tok.shape, BF),
            pltpu.VMEM((2 * images * experts, width), BF),
            pltpu.SemaphoreType.DMA((2, images)),
        ],
        compiler_params=params(16),
        cost_estimate=cost(6 * images * toks * width * experts, 4 * images * toks * width),
        name="logit_grads",
    )(back, in_hbm(tok), in_hbm(cot), disp, comb)


def tokens_kernel(disp, lgrad, sgrad, router, out):
    for n in range(disp.shape[0]):
        left = jnp.concatenate([disp[n].astype(BF), lgrad[n]], axis=0)
        right = jnp.concatenate([sgrad[n], router[...]], axis=0)
        out[n] = mm(left, right, 0, 0).astype(BF)


def token_grads(disp, lgrad, sgrad, router_t):
    images, experts, toks = disp.shape
    width = router_t.shape[1]
    return pl.pallas_call(
        tokens_kernel,
        out_shape=jax.ShapeDtypeStruct((images, toks, width), BF),
        in_specs=[VM] * 4,
        out_specs=VM,
        compiler_params=params(16),
        cost_estimate=cost(4 * images * toks * width * experts, 2 * images * toks * width),
        name="token_grads",
    )(disp, lgrad, sgrad, router_t)


def xor_permute(x, axis, size, mask):
    return lax.ppermute(x, axis, [(i, i ^ mask) for i in range(size)])


def all_sum(x, sizes):
    for axis in ("pair", "expert"):
        size, step = sizes[axis], 1
        while step < size:
            span = 4 if size // step >= 4 else 2
            x = lax.reduce_precision(x, 8, 7)
            sent = x.astype(BF)
            got = [xor_permute(sent, axis, size, step * k) for k in range(1, span)]
            got = [x] + [part.astype(F32) for part in got]
            x = got[0] + got[1]
            if span == 4:
                x = x + (got[2] + got[3])
            step *= span
    return x


def make_per_device(sizes):
    def swap(x):
        return lax.ppermute(x, "pair", [(0, 1), (1, 0)])

    def exchange(x):
        blocks = x.reshape(sizes["expert"], -1, x.shape[1])
        return lax.all_to_all(blocks, "expert", split_axis=0, concat_axis=0, tiled=True).reshape(x.shape)

    def per_device(tokens, router, w_in, w_out, out_grad):
        images = tokens.shape[0]
        send, disp, comb, router_t, held_in, held_out = make_slots(
            tokens, out_grad, router.T, w_in[0], w_out[0]
        )
        mine = exchange(send)
        theirs = swap(mine)
        keep, give, slot_rows, cot_rows, act, hgrad = run_expert(
            mine, theirs, held_in, held_out, images
        )
        got = swap(give)
        joined = join(keep, got, images)
        back = exchange(joined)
        grad_in = mm(slot_rows, hgrad, 0, 0).astype(BF)
        grad_out = mm(act, cot_rows, 0, 0).astype(BF)
        part, lgrad, sgrad = logit_grads(back, tokens, out_grad, disp, comb)
        tokens_grad = token_grads(disp, lgrad, sgrad, router_t)
        router_grad = all_sum(part, sizes).T
        return tokens_grad, grad_in[None], grad_out[None], router_grad

    return per_device


def solution(mesh):
    in_specs = (
        P(("expert", "pair"), None, None),
        P(),
        P("expert", None, "pair"),
        P("expert", "pair", None),
        P(("expert", "pair"), None, None),
    )
    out_specs = (
        P(("expert", "pair"), None, None),
        P("expert", None, "pair"),
        P("expert", "pair", None),
        P(),
    )
    return jax.shard_map(
        make_per_device(dict(mesh.shape)),
        mesh=mesh,
        in_specs=in_specs,
        out_specs=out_specs,
        check_vma=False,
    )
```

profile of v0, /device:TPU:0, one launch (start us, length us, event | category | flops | bytes accessed | tf_op | source)
XLA Modules:
  0.0 77.6 jit_solution(16638235333679474514)
XLA Ops:
  0.6 8.0 %slots.1 = (bf16[384,512]{1,0:T(8,128)(2,1)S(1)}, f32[6,16,196]{2,1,0:T(8,128)S(1)}, f32[6,16,196]{2,1,0:T(8,128)S(1)}, bf16[16,1024]{1,0:T(8,128)(2,1)S(1)}, bf...) custom-call(bf16[6,196,1024]{2,1,0:T(8,128)(2,1)} %tok_hbm.3, bf16[6,196,1024]{2,1,0:T(8,128)(2,1)} %cot_hbm.3, ...), custom_call_target="tpu_custom_call" | custom-call | flops 115605504 | bytes 4816896 | tf_op jit(solution)/shard_map/slots/pallas_call | solution.py:114
  8.6 20.8 %all_to_all.10 = bf16[16,24,512]{2,1,0:T(8,128)(2,1)S(1)} all-to-all(bf16[16,24,512]{2,1,0:T(8,128)(2,1)S(1)} %bitcast.21), channel_id=1, replica_groups=mesh['expert'=16,'pair'=2] {'expert'}, dimensions={0} | all-to-all | bytes 786432 | tf_op jit(solution)/shard_map/all_to_all | solution.py:360
  29.4 0.0 collective-permute-start
  29.4 1.7 %collective-permute-done.theirs = bf16[384,512]{1,0:T(8,128)(2,1)S(1)} collective-permute-done((bf16[384,512]{1,0:T(8,128)(2,1)S(1)}, bf16[384,512]{1,0:T(8,128)(2,1)S(1)}, u32[]{:S(2)}, u32[]{:S(2)}) %collective-permute-start) | collective-permute-done | bytes 393248 | tf_op jit(solution)/shard_map/ppermute | solution.py:356
  31.1 4.8 %expert.1 = (f32[192,1024]{1,0:T(8,128)S(1)}, bf16[192,1024]{1,0:T(8,128)(2,1)S(1)}, bf16[192,1024]{1,0:T(8,128)(2,1)S(1)}, bf16[192,1024]{1,0:T(8,128)(2,1)S(1)...) custom-call(bf16[384,512]{1,0:T(8,128)(2,1)S(1)} %bitcast.20, ...), custom_call_target="tpu_custom_call" | custom-call | flops 3221225472 | bytes 8388608 | tf_op jit(solution)/shard_map/expert/pallas_call | solution.py:191
  35.9 0.2 collective-permute-start.1
  36.1 1.6 %collective-permute-done.1.got = bf16[192,1024]{1,0:T(8,128)(2,1)S(1)} collective-permute-done((bf16[192,1024]{1,0:T(8,128)(2,1)S(1)}, bf16[192,1024]{1,0:T(8,128)(2,1)S(1)}, u32[]{:S(2)}, u32[]{:S(2)}) %collective-permute-start.1) | collective-permute-done | bytes 393248 | tf_op jit(solution)/shard_map/ppermute | solution.py:356
  37.6 0.4 join.1
  38.0 16.3 %all_to_all.11 = bf16[16,24,512]{2,1,0:T(8,128)(2,1)S(1)} all-to-all(bf16[16,24,512]{2,1,0:T(8,128)(2,1)S(1)} %bitcast.17), channel_id=1, replica_groups=mesh['expert'=16,'pair'=2] {'expert'}, dimensions={0} | all-to-all | bytes 786432 | tf_op jit(solution)/shard_map/all_to_all | solution.py:360
  54.3 4.3 %logit_grads.1 = (f32[16,1024]{1,0:T(8,128)S(1)}, bf16[6,16,196]{2,1,0:T(8,128)(2,1)S(1)}, bf16[6,16,1024]{2,1,0:T(8,128)(2,1)S(1)}) custom-call(bf16[384,512]{1,0:T(8,128)(2,1)S(1)} %bitcast.18, bf16[6,196,1024]{2,1,0:T(8,128)(2,1)} %tok_hbm.3, bf16[6,196,1024]{2,1,0:T(8,128)(2,1)} %cot_hbm.3, f32[6,16,196]{2,1,0:T(8,128)S(1)} %get-tuple-element.19.disp, ...), custom_call_target="tpu_custom_call" | custom-call | flops 115605504 | bytes 4816896 | tf_op jit(solution)/shard_map/logit_grads/pallas_call | solution.py:292
  58.6 0.1 collective-permute-start.2
  58.7 1.2 %collective-permute-done.2 = bf16[16,1024]{1,0:T(8,128)(2,1)S(1)} collective-permute-done((bf16[16,1024]{1,0:T(8,128)(2,1)S(1)}, bf16[16,1024]{1,0:T(8,128)(2,1)S(1)}, u32[]{:S(2)}, u32[]{:S(2)}) %collective-permute-start.2) | collective-permute-done | bytes 32800 | tf_op jit(solution)/shard_map/ppermute | solution.py:335
  59.9 0.9 %collective-permute-start.5 = (bf16[16,1024]{1,0:T(8,128)(2,1)S(1)}, bf16[16,1024]{1,0:T(8,128)(2,1)S(1)}, u32[]{:S(2)}, u32[]{:S(2)}) collective-permute-start(bf16[16,1024]{1,0:T(8,128)(2,1)S(1)} %fusion), channel_id=1, source_target_pairs={{0,6},{2,4},{4,2},{6,0},{8,14},{10,12},{12,10},{14,8},{16,22},{18,... | collective-permute-start | bytes 98312 | tf_op jit(solution)/shard_map/ppermute | solution.py:335
  60.8 1.2 %collective-permute-start.4 = (bf16[16,1024]{1,0:T(8,128)(2,1)S(1)}, bf16[16,1024]{1,0:T(8,128)(2,1)S(1)}, u32[]{:S(2)}, u32[]{:S(2)}) collective-permute-start(bf16[16,1024]{1,0:T(8,128)(2,1)S(1)} %fusion), channel_id=1, source_target_pairs={{0,4},{2,6},{4,0},{6,2},{8,12},{10,14},{12,8},{14,10},{16,20},{18,... | collective-permute-start | bytes 98312 | tf_op jit(solution)/shard_map/ppermute | solution.py:335
  62.0 1.5 %collective-permute-start.3 = (bf16[16,1024]{1,0:T(8,128)(2,1)S(1)}, bf16[16,1024]{1,0:T(8,128)(2,1)S(1)}, u32[]{:S(2)}, u32[]{:S(2)}) collective-permute-start(bf16[16,1024]{1,0:T(8,128)(2,1)S(1)} %fusion), channel_id=1, source_target_pairs={{0,2},{2,0},{4,6},{6,4},{8,10},{10,8},{12,14},{14,12},{16,18},{18,... | collective-permute-start | bytes 98312 | tf_op jit(solution)/shard_map/ppermute | solution.py:335
  63.5 3.3 %convert_bitcast_fusion.1 = bf16[1,1024,2048]{2,1,0:T(8,128)(2,1)} fusion(bf16[192,1024]{1,0:T(8,128)(2,1)S(1)} %get-tuple-element.29, bf16[192,2048]{1,0:T(8,128)(2,1)S(1)} %get-tuple-element.30), kind=kOutput, calls=%fused_computation.1 | convolution fusion | flops 807403520 | bytes 5373952 | tf_op jit(solution)/shard_map/dot_general | solution.py:25
  66.8 0.0 collective-permute-done.5
  66.8 0.0 collective-permute-done.4
  66.8 0.0 collective-permute-done.3
  66.8 1.6 %collective-permute-start.8 = (bf16[16,1024]{1,0:T(8,128)(2,1)S(1)}, bf16[16,1024]{1,0:T(8,128)(2,1)S(1)}, u32[]{:S(2)}, u32[]{:S(2)}) collective-permute-start(bf16[16,1024]{1,0:T(8,128)(2,1)S(1)} %fusion.1), channel_id=1, source_target_pairs={{0,24},{2,26},{4,28},{6,30},{8,16},{10,18},{12,20},{14,22},{16,8},... | collective-permute-start | bytes 98312 | tf_op jit(solution)/shard_map/ppermute | solution.py:335
  68.4 1.0 %collective-permute-start.7 = (bf16[16,1024]{1,0:T(8,128)(2,1)S(1)}, bf16[16,1024]{1,0:T(8,128)(2,1)S(1)}, u32[]{:S(2)}, u32[]{:S(2)}) collective-permute-start(bf16[16,1024]{1,0:T(8,128)(2,1)S(1)} %fusion.1), channel_id=1, source_target_pairs={{0,16},{2,18},{4,20},{6,22},{8,24},{10,26},{12,28},{14,30},{16,0},... | collective-permute-start | bytes 98312 | tf_op jit(solution)/shard_map/ppermute | solution.py:335
  69.4 1.8 %collective-permute-start.6 = (bf16[16,1024]{1,0:T(8,128)(2,1)S(1)}, bf16[16,1024]{1,0:T(8,128)(2,1)S(1)}, u32[]{:S(2)}, u32[]{:S(2)}) collective-permute-start(bf16[16,1024]{1,0:T(8,128)(2,1)S(1)} %fusion.1), channel_id=1, source_target_pairs={{0,8},{2,10},{4,12},{6,14},{8,0},{10,2},{12,4},{14,6},{16,24},{18,... | collective-permute-start | bytes 98312 | tf_op jit(solution)/shard_map/ppermute | solution.py:335
  71.3 3.3 %convert_bitcast_fusion = bf16[1,2048,1024]{2,1,0:T(8,128)(2,1)} fusion(bf16[192,2048]{1,0:T(8,128)(2,1)S(1)} %get-tuple-element.31, bf16[192,1024]{1,0:T(8,128)(2,1)S(1)} %get-tuple-element.32), kind=kOutput, calls=%fused_computation | convolution fusion | flops 807403520 | bytes 5373952 | tf_op jit(solution)/shard_map/dot_general | solution.py:25
  74.6 2.3 %token_grads.1 = bf16[6,196,1024]{2,1,0:T(8,128)(2,1)} custom-call(f32[6,16,196]{2,1,0:T(8,128)S(1)} %get-tuple-element.19.disp, bf16[6,16,196]{2,1,0:T(8,128)(2,1)S(1)} %get-tuple-element.26.lgrad, bf16[6,16,1024]{2,1,0:T(8,128)(2,1)S(1)} %get-tuple-element.27.sgrad, bf16[16,1024]{1,0:T(8,128)(2,1)S(1)} %get-tuple-element.28.router), custom_call_target="tpu_custom_call" | custom-call | flops 77070336 | bytes 2408448 | tf_op jit(solution)/shard_map/token_grads/pallas_call | solution.py:323
  76.9 0.0 collective-permute-done.8
  76.9 0.0 collective-permute-done.7
  76.9 0.0 collective-permute-done.6
  76.9 0.7 add_bitcast_fusion
  (3 shorter events, 0.1 us)
Async XLA Ops:
  29.4 1.7 %collective-permute-start = (bf16[384,512]{1,0:T(8,128)(2,1)S(1)}, bf16[384,512]{1,0:T(8,128)(2,1)S(1)}, u32[]{:S(2)}, u32[]{:S(2)}) collective-permute-start(bf16[384,512]{1,0:T(8,128)(2,1)S(1)} %bitcast.19), channel_id=1, source_target_pairs={{0,1},{1,0},{2,3},{3,2},{4,5},{5,4},{6,7},{7,6},{8,9},{9,8},{10,11... | collective-permute-start | bytes 1179656 | tf_op jit(solution)/shard_map/ppermute | solution.py:356
  35.9 1.8 %collective-permute-start.1 = (bf16[192,1024]{1,0:T(8,128)(2,1)S(1)}, bf16[192,1024]{1,0:T(8,128)(2,1)S(1)}, u32[]{:S(2)}, u32[]{:S(2)}) collective-permute-start(bf16[192,1024]{1,0:T(8,128)(2,1)S(1)} %get-tuple-element.24), channel_id=1, source_target_pairs={{0,1},{1,0},{2,3},{3,2},{4,5},{5,4},{6,7},{7,6},{8,9},{9,8},{10,11... | collective-permute-start | bytes 1179656 | tf_op jit(solution)/shard_map/ppermute | solution.py:356
  58.6 1.3 %collective-permute-start.2 = (bf16[16,1024]{1,0:T(8,128)(2,1)S(1)}, bf16[16,1024]{1,0:T(8,128)(2,1)S(1)}, u32[]{:S(2)}, u32[]{:S(2)}) collective-permute-start(bf16[16,1024]{1,0:T(8,128)(2,1)S(1)} %reduce-precision_convert_fusion), channel_id=1, source_target_pairs={{0,1},{1,0},{2,3},{3,2},{4,5},{5,4},{6,7},{7,6},{8,9},{9,8},{10,11... | collective-permute-start | bytes 98312 | tf_op jit(solution)/shard_map/ppermute | solution.py:335
  59.9 6.9 %collective-permute-start.5 = (bf16[16,1024]{1,0:T(8,128)(2,1)S(1)}, bf16[16,1024]{1,0:T(8,128)(2,1)S(1)}, u32[]{:S(2)}, u32[]{:S(2)}) collective-permute-start(bf16[16,1024]{1,0:T(8,128)(2,1)S(1)} %fusion), channel_id=1, source_target_pairs={{0,6},{2,4},{4,2},{6,0},{8,14},{10,12},{12,10},{14,8},{16,22},{18,... | collective-permute-start | bytes 98312 | tf_op jit(solution)/shard_map/ppermute | solution.py:335
  60.8 6.0 %collective-permute-start.4 = (bf16[16,1024]{1,0:T(8,128)(2,1)S(1)}, bf16[16,1024]{1,0:T(8,128)(2,1)S(1)}, u32[]{:S(2)}, u32[]{:S(2)}) collective-permute-start(bf16[16,1024]{1,0:T(8,128)(2,1)S(1)} %fusion), channel_id=1, source_target_pairs={{0,4},{2,6},{4,0},{6,2},{8,12},{10,14},{12,8},{14,10},{16,20},{18,... | collective-permute-start | bytes 98312 | tf_op jit(solution)/shard_map/ppermute | solution.py:335
  62.0 4.8 %collective-permute-start.3 = (bf16[16,1024]{1,0:T(8,128)(2,1)S(1)}, bf16[16,1024]{1,0:T(8,128)(2,1)S(1)}, u32[]{:S(2)}, u32[]{:S(2)}) collective-permute-start(bf16[16,1024]{1,0:T(8,128)(2,1)S(1)} %fusion), channel_id=1, source_target_pairs={{0,2},{2,0},{4,6},{6,4},{8,10},{10,8},{12,14},{14,12},{16,18},{18,... | collective-permute-start | bytes 98312 | tf_op jit(solution)/shard_map/ppermute | solution.py:335
  66.8 10.1 %collective-permute-start.8 = (bf16[16,1024]{1,0:T(8,128)(2,1)S(1)}, bf16[16,1024]{1,0:T(8,128)(2,1)S(1)}, u32[]{:S(2)}, u32[]{:S(2)}) collective-permute-start(bf16[16,1024]{1,0:T(8,128)(2,1)S(1)} %fusion.1), channel_id=1, source_target_pairs={{0,24},{2,26},{4,28},{6,30},{8,16},{10,18},{12,20},{14,22},{16,8},... | collective-permute-start | bytes 98312 | tf_op jit(solution)/shard_map/ppermute | solution.py:335
  68.4 8.5 %collective-permute-start.7 = (bf16[16,1024]{1,0:T(8,128)(2,1)S(1)}, bf16[16,1024]{1,0:T(8,128)(2,1)S(1)}, u32[]{:S(2)}, u32[]{:S(2)}) collective-permute-start(bf16[16,1024]{1,0:T(8,128)(2,1)S(1)} %fusion.1), channel_id=1, source_target_pairs={{0,16},{2,18},{4,20},{6,22},{8,24},{10,26},{12,28},{14,30},{16,0},... | collective-permute-start | bytes 98312 | tf_op jit(solution)/shard_map/ppermute | solution.py:335
  69.4 7.4 %collective-permute-start.6 = (bf16[16,1024]{1,0:T(8,128)(2,1)S(1)}, bf16[16,1024]{1,0:T(8,128)(2,1)S(1)}, u32[]{:S(2)}, u32[]{:S(2)}) collective-permute-start(bf16[16,1024]{1,0:T(8,128)(2,1)S(1)} %fusion.1), channel_id=1, source_target_pairs={{0,8},{2,10},{4,12},{6,14},{8,0},{10,2},{12,4},{14,6},{16,24},{18,... | collective-permute-start | bytes 98312 | tf_op jit(solution)/shard_map/ppermute | solution.py:335
where the time goes:
time: 77.8 us; the launch traced here: 77.6 us
  blocking collectives  37.1 us (48%)
  Pallas kernels  19.7 us (25%)
  starting transfers between devices  8.28 us (11%)
  matrix products  6.62 us (9%)
  waiting for transfers between devices  4.52 us (6%)
    all_to_all x2, blocking collectives, exchange(): lax.all_to_all(blocks, 'expert', split_axis=0, concat_axis=0, tiled=True)  37.1 us
    ppermute x7, starting transfers between devices, xor_permute(): return lax.ppermute(x, axis, [(i, i ^ mask) for i in range(size)])  8.08 us
    pallas_call x1, Pallas kernels, make_slots(): pl.pallas_call(functools.partial(slots_kernel, pieces), out_shape=(jax.Sh...  7.96 us
    dot_general x2, matrix products, mm(): lax.dot_general(a, b, (((da,), (db,)), ((), ())), preferred_element_type=...  6.62 us
    pallas_call x1, Pallas kernels, run_expert(): pl.pallas_call(functools.partial(expert_kernel, pieces, images), out_shap...  4.76 us
    pallas_call x1, Pallas kernels, logit_grads(): pl.pallas_call(functools.partial(logits_kernel, pieces), out_shape=(jax.S...  4.26 us
    ppermute x2, waiting for transfers between devices, swap(): return lax.ppermute(x, 'pair', [(0, 1), (1, 0)])  3.31 us
    pallas_call x1, Pallas kernels, token_grads(): pl.pallas_call(tokens_kernel, out_shape=jax.ShapeDtypeStruct((images, tok...  2.29 us
  transfers between devices with their start and end apart: 9, of which 3 were waited for; matrix products, arithmetic and copies ran while one was open for 9% of the time, Pallas kernels for 3%

commit v1 on v0

--- a/solution.py
+++ b/solution.py
@@ -58,120 +58,136 @@
     return jnp.where(row == wanted, 1.0, 0.0).astype(BF)
 
 
+def part_copy(source, target, sems, i):
+    size = source.shape[0] // sems.shape[0]
+    rows = pl.ds(i * size, size)
+    return pltpu.make_async_copy(source.at[rows], target.at[rows], sems.at[i])
+
+
+def start_parts(*triples):
+    def body(i, carry):
+        for source, target, sems in triples:
+            part_copy(source, target, sems, i).start()
+        return carry
+
+    lax.fori_loop(0, triples[0][2].shape[0], body, 0)
+
+
+def wait_parts(source, target, sems, some=None):
+    for i in range(sems.shape[0]) if some is None else some:
+        part_copy(source, target, sems, i).wait()
+
+
 def slots_kernel(
-    pieces, tok_hbm, cot_hbm, router_hbm, first, second,
-    send, disp, comb, router, held_first, held_second,
-    tok, cot, rows, sems, more_sems,
+    pieces, chunk, tok_hbm, cot_hbm, router_hbm, weight,
+    send, disp, comb, router, held,
+    tok, cot, rows, tok_sems, cot_sems, router_sem, held_sems,
 ):
     images, _, width = tok_hbm.shape
-    experts = router.shape[0]
-    router_copy = pltpu.make_async_copy(router_hbm, router, more_sems.at[0])
+    experts = router_hbm.shape[0]
+    router_copy = pltpu.make_async_copy(router_hbm, router, router_sem)
     router_copy.start()
-    held = (
-        pltpu.make_async_copy(first, held_first, more_sems.at[1]),
-        pltpu.make_async_copy(second, held_second, more_sems.at[2]),
-    )
+    start_parts((tok_hbm, tok, tok_sems))
+    start_parts((cot_hbm, cot, cot_sems))
+    router_copy.wait()
+    mixes = []
+    for start in range(0, images, chunk):
+        some = range(start, min(start + chunk, images))
+        wait_parts(tok_hbm, tok, tok_sems, some)
+        if start + chunk >= images:
+            start_parts((weight, held, held_sems))
+        logits = [mm(router[...], tok[n], 1, 1) for n in some]
+        down = [jnp.exp(x - jnp.max(x, axis=1, keepdims=True)) for x in logits]
+        across = [jnp.exp(x - jnp.max(x, axis=0, keepdims=True)) for x in logits]
+        down = [x / jnp.sum(x, axis=1, keepdims=True) for x in down]
+        across = [x / jnp.sum(x, axis=0, keepdims=True) for x in across]
+        for n, dispatch, combine in zip(some, down, across):
+            disp[n] = dispatch
+            comb[n] = combine
+            mixes.append(combine.astype(BF))
+            rows[pl.ds(n * experts, experts), :] = mm(dispatch.astype(BF), tok[n]).astype(BF)
+    wait_parts(cot_hbm, cot, cot_sems)
+    for n in range(images):
+        rows[pl.ds((images + n) * experts, experts), :] = mm(mixes[n], cot[n]).astype(BF)
     part = width // pieces
-    copies = []
-    for n in range(images):
-        pair = (
-            pltpu.make_async_copy(tok_hbm.at[n], tok.at[n], sems.at[0, n]),
-            pltpu.make_async_copy(cot_hbm.at[n], cot.at[n], sems.at[1, n]),
-        )
-        pair[0].start()
-        pair[1].start()
-        copies.append(pair)
-    for copy in held:
-        copy.start()
-    router_copy.wait()
-    for n in range(images):
-        copies[n][0].wait()
-        logits = mm(router[...], tok[n], 1, 1)
-        top = jnp.exp(logits - jnp.max(logits, axis=1, keepdims=True))
-        dispatch = top / jnp.sum(top, axis=1, keepdims=True)
-        top = jnp.exp(logits - jnp.max(logits, axis=0, keepdims=True))
-        combine = top / jnp.sum(top, axis=0, keepdims=True)
-        disp[n] = dispatch
-        comb[n] = combine
-        rows[pl.ds(n * experts, experts), :] = mm(dispatch.astype(BF), tok[n]).astype(BF)
-        copies[n][1].wait()
-        rows[pl.ds((images + n) * experts, experts), :] = mm(combine.astype(BF), cot[n]).astype(BF)
-    kind = 2 * images
     total = None
     for count in range(pieces):
-        term = mm(spread(kind, count, pieces, experts), rows[:, count * part : (count + 1) * part])
+        pick = spread(2 * images, count, pieces, experts)
+        term = mm(pick, rows[:, count * part : (count + 1) * part])
         total = term if total is None else total + term
     send[...] = total.astype(BF)
-    for copy in held:
-        copy.wait()
-
-
-def make_slots(tokens, out_grad, router_t, first, second):
+    wait_parts(weight, held, held_sems)
+
+
+def make_slots(tokens, out_grad, router_t, weight):
     images, toks, width = tokens.shape
     experts = router_t.shape[0]
     pieces = pieces_of(images)
-    block = 2 * images * pieces
     return pl.pallas_call(
-        functools.partial(slots_kernel, pieces),
+        functools.partial(slots_kernel, pieces, 3),
         out_shape=(
-            jax.ShapeDtypeStruct((experts * block, width // pieces), BF),
+            pltpu.VMEM((2 * images * experts * pieces, width // pieces), BF),
             pltpu.VMEM((images, experts, toks), F32),
             pltpu.VMEM((images, experts, toks), F32),
             pltpu.VMEM(router_t.shape, BF),
-            pltpu.VMEM(first.shape, BF),
-            pltpu.VMEM(second.shape, BF),
+            pltpu.VMEM(weight.shape, BF),
         ),
-        in_specs=[HBM] * 5,
-        out_specs=(VM,) * 6,
+        in_specs=[HBM] * 4,
+        out_specs=(VM,) * 5,
         scratch_shapes=[
             pltpu.VMEM(tokens.shape, BF),
             pltpu.VMEM(tokens.shape, BF),
             pltpu.VMEM((2 * images * experts, width), BF),
-            pltpu.SemaphoreType.DMA((2, images)),
-            pltpu.SemaphoreType.DMA((3,)),
+            pltpu.SemaphoreType.DMA((images,)),
+            pltpu.SemaphoreType.DMA((images,)),
+            pltpu.SemaphoreType.DMA,
+            pltpu.SemaphoreType.DMA((8,)),
         ],
         compiler_params=params(16),
         cost_estimate=cost(6 * images * toks * width * experts, 4 * images * toks * width),
         name="slots",
-    )(*(in_hbm(x) for x in (tokens, out_grad, router_t, first, second)))
+    )(*(in_hbm(x) for x in (tokens, out_grad, router_t, weight)))
 
 
 def expert_kernel(
-    pieces, images, mine, theirs, w_in, w_out, keep, give, slot, cot, act, hgrad
+    pieces, images, mine, theirs, w_in, w_out_hbm, keep, give, slot, cot, act, hgrad, slope, w_out, sems
 ):
+    start_parts((w_out_hbm, w_out, sems))
     half = mine.shape[0] // (2 * pieces)
     part = mine.shape[1]
     width = pieces * part
     hidden = w_in.shape[1]
     kind = 2 * images
     groups = mine.shape[0] // (pieces * kind)
-    for count in range(pieces):
-        pick = gather(
-            kind,
-            count,
-            pieces,
-            groups,
-            lambda place, source: jnp.where(
-                place >= images,
-                groups * images + source * images + place - images,
-                source * images + place,
-            ),
-        )
-        columns = slice(count * part, (count + 1) * part)
-        for base, ref in ((0, mine), (half, theirs)):
-            both = mm(pick, ref[...]).astype(BF)
-            slot[base : base + half, columns] = both[:half]
-            cot[base : base + half, columns] = both[half:]
+    some = math.gcd(groups, 8)
+    block = pieces * kind
+    column = lax.broadcasted_iota(jnp.int32, (1, some * block), 1)
+    source = column // block
+    place = column - source * block
+    series = place // images
+    wanted = (series * some + source) * images + place - series * images
+    row = lax.broadcasted_iota(jnp.int32, (some * block, some * block), 0)
+    pick = jnp.where(row == wanted, 1.0, 0.0).astype(BF)
+    size = some * images
+    for base, ref in ((0, mine), (half, theirs)):
+        for group in range(groups // some):
+            both = mm(pick, ref[group * some * block : (group + 1) * some * block, :]).astype(BF)
+            at = base + group * size
+            for count in range(pieces):
+                columns = slice(count * part, (count + 1) * part)
+                slot[at : at + size, columns] = both[2 * count * size : (2 * count + 1) * size]
+                cot[at : at + size, columns] = both[(2 * count + 1) * size : (2 * count + 2) * size]
     step = 256
     for f in range(0, hidden, step):
         x = mm(slot[...], w_in[:, f : f + step])
+        inner = x * (ROOT * CUBE * (x * x) + ROOT)
+        up = 0.5 * jnp.tanh(inner) + 0.5
+        act[:, f : f + step] = (x * up).astype(BF)
+        slope[:, f : f + step] = up + up * (1.0 - up) * (6.0 * inner - 4.0 * ROOT * x)
+    wait_parts(w_out_hbm, w_out, sems)
+    for f in range(0, hidden, step):
         g = mm(cot[...], w_out[f : f + step, :], 1, 1)
-        square = x * x
-        t = jnp.tanh(ROOT * x * (1.0 + CUBE * square))
-        up = 0.5 + 0.5 * t
-        act[:, f : f + step] = (x * up).astype(BF)
-        slope = up + x * (0.5 * ROOT) * (1.0 - t * t) * (1.0 + (3.0 * CUBE) * square)
-        hgrad[:, f : f + step] = (g * slope).astype(BF)
+        hgrad[:, f : f + step] = (g * slope[:, f : f + step]).astype(BF)
     step = 256
     for c in range(0, width, step):
         columns = slice(c, c + step)
@@ -198,12 +214,17 @@
             jax.ShapeDtypeStruct((rows, hidden), BF),
             jax.ShapeDtypeStruct((rows, hidden), BF),
         ),
-        in_specs=[VM] * 4,
+        in_specs=[VM, VM, VM, HBM],
         out_specs=(VM,) * 6,
+        scratch_shapes=[
+            pltpu.VMEM((rows, hidden), F32),
+            pltpu.VMEM(w_out.shape, BF),
+            pltpu.SemaphoreType.DMA((8,)),
+        ],
         compiler_params=params(32),
         cost_estimate=cost(8 * rows * width * hidden, 4 * width * hidden),
         name="expert",
-    )(mine, theirs, w_in, w_out)
+    )(mine, theirs, w_in, in_hbm(w_out))
 
 
 def join_kernel(pieces, images, keep, got, send):
@@ -247,18 +268,10 @@
 
 
 def logits_kernel(
-    pieces, back, tok_hbm, cot_hbm, disp, comb, part_out, lgrad, sgrad, tok, cot, rows, sems
+    pieces, back, tok_hbm, cot, disp, comb, part_out, lgrad, sgrad, tok, rows, sems
 ):
     images, experts, _ = disp.shape
-    copies = []
-    for n in range(images):
-        pair = (
-            pltpu.make_async_copy(cot_hbm.at[n], cot.at[n], sems.at[1, n]),
-            pltpu.make_async_copy(tok_hbm.at[n], tok.at[n], sems.at[0, n]),
-        )
-        pair[0].start()
-        pair[1].start()
-        copies.append(pair)
+    start_parts((tok_hbm, tok, sems))
     kind = 2 * images
     part = back.shape[1]
     for count in range(pieces):
@@ -266,21 +279,19 @@
             kind, count, pieces, experts, lambda place, expert: place * experts + expert
         )
         rows[:, count * part : (count + 1) * part] = mm(pick, back[...]).astype(BF)
+    every = range(images)
+    c = [mm(rows[n * experts : (n + 1) * experts, :], cot[n], 1, 1) for n in every]
+    c = [comb[n] * (x - jnp.sum(comb[n] * x, axis=0, keepdims=True)) for n, x in zip(every, c)]
+    wait_parts(tok_hbm, tok, sems)
+    slots = [rows[(images + n) * experts : (images + n + 1) * experts, :] for n in every]
+    d = [mm(x, tok[n], 1, 1) for n, x in zip(every, slots)]
+    d = [disp[n] * (x - jnp.sum(disp[n] * x, axis=1, keepdims=True)) for n, x in zip(every, d)]
+    both = [(x + y).astype(BF) for x, y in zip(c, d)]
     total = None
-    for n in range(images):
-        combine = comb[n]
-        dispatch = disp[n]
-        copies[n][0].wait()
-        copies[n][1].wait()
-        slot = rows[(images + n) * experts : (images + n + 1) * experts, :]
-        c = mm(rows[n * experts : (n + 1) * experts, :], cot[n], 1, 1)
-        d = mm(slot, tok[n], 1, 1)
-        c = combine * (c - jnp.sum(combine * c, axis=0, keepdims=True))
-        d = dispatch * (d - jnp.sum(dispatch * d, axis=1, keepdims=True))
-        both = (c + d).astype(BF)
-        lgrad[n] = both
-        sgrad[n] = slot
-        term = mm(both, tok[n])
+    for n in every:
+        lgrad[n] = both[n]
+        sgrad[n] = slots[n]
+        term = mm(both[n], tok[n])
         total = term if total is None else total + term
     part_out[...] = total
 
@@ -296,18 +307,17 @@
             jax.ShapeDtypeStruct((images, experts, toks), BF),
             jax.ShapeDtypeStruct((images, experts, width), BF),
         ),
-        in_specs=[VM, HBM, HBM, VM, VM],
+        in_specs=[VM, HBM, VM, VM, VM],
         out_specs=(VM,) * 3,
         scratch_shapes=[
             pltpu.VMEM(tok.shape, BF),
-            pltpu.VMEM(tok.shape, BF),
             pltpu.VMEM((2 * images * experts, width), BF),
-            pltpu.SemaphoreType.DMA((2, images)),
+            pltpu.SemaphoreType.DMA((images,)),
         ],
         compiler_params=params(16),
         cost_estimate=cost(6 * images * toks * width * experts, 4 * images * toks * width),
         name="logit_grads",
-    )(back, in_hbm(tok), in_hbm(cot), disp, comb)
+    )(back, in_hbm(tok), cot, disp, comb)
 
 
 def tokens_kernel(disp, lgrad, sgrad, router, out):
@@ -361,13 +371,11 @@
 
     def per_device(tokens, router, w_in, w_out, out_grad):
         images = tokens.shape[0]
-        send, disp, comb, router_t, held_in, held_out = make_slots(
-            tokens, out_grad, router.T, w_in[0], w_out[0]
-        )
+        send, disp, comb, router_t, held_in = make_slots(tokens, out_grad, router.T, w_in[0])
         mine = exchange(send)
         theirs = swap(mine)
         keep, give, slot_rows, cot_rows, act, hgrad = run_expert(
-            mine, theirs, held_in, held_out, images
+            mine, theirs, held_in, w_out[0], images
         )
         got = swap(give)
         joined = join(keep, got, images)

time: 77.8 us -> 74.1 us (0.952)
  Pallas kernels: 19.7 us -> 15.9 us
    pallas_call x1, Pallas kernels: 7.96 us -> 4.53 us  [make_slots(): pl.pallas_call(functools.partial(slots_kernel, pieces, 3), out_shape=(plt...]
    pallas_call x1, Pallas kernels: 4.26 us -> 2.8 us  [logit_grads(): pl.pallas_call(functools.partial(logits_kernel, pieces), out_shape=(jax.S...]
    pallas_call x1, Pallas kernels: 4.76 us -> 5.92 us  [run_expert(): pl.pallas_call(functools.partial(expert_kernel, pieces, images), out_shap...]
where the time goes in v1:
time: 74.1 us; the launch traced here: 73.8 us
  blocking collectives  37.1 us (50%)
  Pallas kernels  15.9 us (21%)
  starting transfers between devices  8.29 us (11%)
  matrix products  6.63 us (9%)
  waiting for transfers between devices  4.51 us (6%)
    all_to_all x2, blocking collectives, exchange(): lax.all_to_all(blocks, 'expert', split_axis=0, concat_axis=0, tiled=True)  37.1 us
    ppermute x7, starting transfers between devices, xor_permute(): return lax.ppermute(x, axis, [(i, i ^ mask) for i in range(size)])  8.08 us
    dot_general x2, matrix products, mm(): lax.dot_general(a, b, (((da,), (db,)), ((), ())), preferred_element_type=...  6.63 us
    pallas_call x1, Pallas kernels, run_expert(): pl.pallas_call(functools.partial(expert_kernel, pieces, images), out_shap...  5.92 us
    pallas_call x1, Pallas kernels, make_slots(): pl.pallas_call(functools.partial(slots_kernel, pieces, 3), out_shape=(plt...  4.53 us
    ppermute x2, waiting for transfers between devices, swap(): return lax.ppermute(x, 'pair', [(0, 1), (1, 0)])  3.3 us
    pallas_call x1, Pallas kernels, logit_grads(): pl.pallas_call(functools.partial(logits_kernel, pieces), out_shape=(jax.S...  2.8 us
    pallas_call x1, Pallas kernels, token_grads(): pl.pallas_call(tokens_kernel, out_shape=jax.ShapeDtypeStruct((images, tok...  2.29 us
  transfers between devices with their start and end apart: 9, of which 3 were waited for; matrix products, arithmetic and copies ran while one was open for 9% of the time, Pallas kernels for 3%

profile of v1, /device:TPU:0, one launch (start us, length us, event | category | flops | bytes accessed | tf_op | source)
XLA Modules:
  0.0 73.8 jit_solution(15566945971185641605)
XLA Ops:
  0.6 4.5 %slots.1 = (bf16[384,512]{1,0:T(8,128)(2,1)S(1)}, f32[6,16,196]{2,1,0:T(8,128)S(1)}, f32[6,16,196]{2,1,0:T(8,128)S(1)}, bf16[16,1024]{1,0:T(8,128)(2,1)S(1)}, bf16[1024,2048]{1,0:T(8,128)(2,1)S(1)}) custom-call(bf16[6,196,1024]{2,1,0:T(8,128)(2,1)} %tok_hbm.3, bf16[6,196,1024]{2,1,0:T(8,128)(2,1)} %cot.1, bf16[16,1024]{1,0:T(8,128)(2,1)} %bitcast.23, ...), custom_call_target="tpu_custom_call" | custom-call | flops 115605504 | bytes 4816896 | tf_op jit(solution)/shard_map/slots/pallas_call | solution.py:126
  5.2 20.8 %all_to_all.10 = bf16[16,24,512]{2,1,0:T(8,128)(2,1)S(1)} all-to-all(bf16[16,24,512]{2,1,0:T(8,128)(2,1)S(1)} %bitcast.21), channel_id=1, replica_groups=mesh['expert'=16,'pair'=2] {'expert'}, dimensions={0} | all-to-all | bytes 786432 | tf_op jit(solution)/shard_map/all_to_all | solution.py:370
  25.9 0.0 collective-permute-start
  25.9 1.7 %collective-permute-done.theirs = bf16[384,512]{1,0:T(8,128)(2,1)S(1)} collective-permute-done((bf16[384,512]{1,0:T(8,128)(2,1)S(1)}, bf16[384,512]{1,0:T(8,128)(2,1)S(1)}, u32[]{:S(2)}, u32[]{:S(2)}) %collective-permute-start) | collective-permute-done | bytes 393248 | tf_op jit(solution)/shard_map/ppermute | solution.py:366
  27.7 0.0 copy-start
  27.7 5.9 %expert.1 = (f32[192,1024]{1,0:T(8,128)S(1)}, bf16[192,1024]{1,0:T(8,128)(2,1)S(1)}, bf16[192,1024]{1,0:T(8,128)(2,1)S(1)}, bf16[192,1024]{1,0:T(8,128)(2,1)S(1)...) custom-call(bf16[384,512]{1,0:T(8,128)(2,1)S(1)} %bitcast.20, ...), custom_call_target="tpu_custom_call" | custom-call | flops 3221225472 | bytes 8388608 | tf_op jit(solution)/shard_map/expert/pallas_call | solution.py:207
  33.6 0.2 collective-permute-start.1
  33.8 1.6 %collective-permute-done.1.got = bf16[192,1024]{1,0:T(8,128)(2,1)S(1)} collective-permute-done((bf16[192,1024]{1,0:T(8,128)(2,1)S(1)}, bf16[192,1024]{1,0:T(8,128)(2,1)S(1)}, u32[]{:S(2)}, u32[]{:S(2)}) %collective-permute-start.1) | collective-permute-done | bytes 393248 | tf_op jit(solution)/shard_map/ppermute | solution.py:366
  35.4 0.4 join.1
  35.8 16.3 %all_to_all.11 = bf16[16,24,512]{2,1,0:T(8,128)(2,1)S(1)} all-to-all(bf16[16,24,512]{2,1,0:T(8,128)(2,1)S(1)} %bitcast.17), channel_id=1, replica_groups=mesh['expert'=16,'pair'=2] {'expert'}, dimensions={0} | all-to-all | bytes 786432 | tf_op jit(solution)/shard_map/all_to_all | solution.py:370
  52.1 0.0 copy-done
  52.1 2.8 %logit_grads.1 = (f32[16,1024]{1,0:T(8,128)S(1)}, bf16[6,16,196]{2,1,0:T(8,128)(2,1)S(1)}, bf16[6,16,1024]{2,1,0:T(8,128)(2,1)S(1)}) custom-call(bf16[384,512]{1,0:T(8,128)(2,1)S(1)} %bitcast.18, bf16[6,196,1024]{2,1,0:T(8,128)(2,1)} %tok_hbm.3, bf16[6,196,1024]{2,1,0:T(8,128)(2,1)S(1)} %copy-done, f32[6,16,196]{2,1,0:T(8,128)S(1)} %get-tuple-element.18.disp, ...), custom_call_target="tpu_custom_call" | custom-call | flops 115605504 | bytes 4816896 | tf_op jit(solution)/shard_map/logit_grads/pallas_call | solution.py:303
  54.9 0.1 collective-permute-start.2
  55.0 1.2 %collective-permute-done.2 = bf16[16,1024]{1,0:T(8,128)(2,1)S(1)} collective-permute-done((bf16[16,1024]{1,0:T(8,128)(2,1)S(1)}, bf16[16,1024]{1,0:T(8,128)(2,1)S(1)}, u32[]{:S(2)}, u32[]{:S(2)}) %collective-permute-start.2) | collective-permute-done | bytes 32800 | tf_op jit(solution)/shard_map/ppermute | solution.py:345
  56.2 0.9 %collective-permute-start.5 = (bf16[16,1024]{1,0:T(8,128)(2,1)S(1)}, bf16[16,1024]{1,0:T(8,128)(2,1)S(1)}, u32[]{:S(2)}, u32[]{:S(2)}) collective-permute-start(bf16[16,1024]{1,0:T(8,128)(2,1)S(1)} %fusion), channel_id=1, source_target_pairs={{0,6},{2,4},{4,2},{6,0},{8,14},{10,12},{12,10},{14,8},{16,22},{18,... | collective-permute-start | bytes 98312 | tf_op jit(solution)/shard_map/ppermute | solution.py:345
  57.1 1.2 %collective-permute-start.4 = (bf16[16,1024]{1,0:T(8,128)(2,1)S(1)}, bf16[16,1024]{1,0:T(8,128)(2,1)S(1)}, u32[]{:S(2)}, u32[]{:S(2)}) collective-permute-start(bf16[16,1024]{1,0:T(8,128)(2,1)S(1)} %fusion), channel_id=1, source_target_pairs={{0,4},{2,6},{4,0},{6,2},{8,12},{10,14},{12,8},{14,10},{16,20},{18,... | collective-permute-start | bytes 98312 | tf_op jit(solution)/shard_map/ppermute | solution.py:345
  58.3 1.5 %collective-permute-start.3 = (bf16[16,1024]{1,0:T(8,128)(2,1)S(1)}, bf16[16,1024]{1,0:T(8,128)(2,1)S(1)}, u32[]{:S(2)}, u32[]{:S(2)}) collective-permute-start(bf16[16,1024]{1,0:T(8,128)(2,1)S(1)} %fusion), channel_id=1, source_target_pairs={{0,2},{2,0},{4,6},{6,4},{8,10},{10,8},{12,14},{14,12},{16,18},{18,... | collective-permute-start | bytes 98312 | tf_op jit(solution)/shard_map/ppermute | solution.py:345
  59.7 3.3 %convert_bitcast_fusion.1 = bf16[1,1024,2048]{2,1,0:T(8,128)(2,1)} fusion(bf16[192,1024]{1,0:T(8,128)(2,1)S(1)} %get-tuple-element.27, bf16[192,2048]{1,0:T(8,128)(2,1)S(1)} %get-tuple-element.28), kind=kOutput, calls=%fused_computation.1 | convolution fusion | flops 807403520 | bytes 5373952 | tf_op jit(solution)/shard_map/dot_general | solution.py:25
  63.0 0.0 collective-permute-done.5
  63.0 0.0 collective-permute-done.4
  63.0 0.0 collective-permute-done.3
  63.1 1.6 %collective-permute-start.8 = (bf16[16,1024]{1,0:T(8,128)(2,1)S(1)}, bf16[16,1024]{1,0:T(8,128)(2,1)S(1)}, u32[]{:S(2)}, u32[]{:S(2)}) collective-permute-start(bf16[16,1024]{1,0:T(8,128)(2,1)S(1)} %fusion.1), channel_id=1, source_target_pairs={{0,24},{2,26},{4,28},{6,30},{8,16},{10,18},{12,20},{14,22},{16,8},... | collective-permute-start | bytes 98312 | tf_op jit(solution)/shard_map/ppermute | solution.py:345
  64.7 1.0 %collective-permute-start.7 = (bf16[16,1024]{1,0:T(8,128)(2,1)S(1)}, bf16[16,1024]{1,0:T(8,128)(2,1)S(1)}, u32[]{:S(2)}, u32[]{:S(2)}) collective-permute-start(bf16[16,1024]{1,0:T(8,128)(2,1)S(1)} %fusion.1), channel_id=1, source_target_pairs={{0,16},{2,18},{4,20},{6,22},{8,24},{10,26},{12,28},{14,30},{16,0},... | collective-permute-start | bytes 98312 | tf_op jit(solution)/shard_map/ppermute | solution.py:345
  65.7 1.8 %collective-permute-start.6 = (bf16[16,1024]{1,0:T(8,128)(2,1)S(1)}, bf16[16,1024]{1,0:T(8,128)(2,1)S(1)}, u32[]{:S(2)}, u32[]{:S(2)}) collective-permute-start(bf16[16,1024]{1,0:T(8,128)(2,1)S(1)} %fusion.1), channel_id=1, source_target_pairs={{0,8},{2,10},{4,12},{6,14},{8,0},{10,2},{12,4},{14,6},{16,24},{18,... | collective-permute-start | bytes 98312 | tf_op jit(solution)/shard_map/ppermute | solution.py:345
  67.5 3.3 %convert_bitcast_fusion = bf16[1,2048,1024]{2,1,0:T(8,128)(2,1)} fusion(bf16[192,2048]{1,0:T(8,128)(2,1)S(1)} %get-tuple-element.29, bf16[192,1024]{1,0:T(8,128)(2,1)S(1)} %get-tuple-element.30), kind=kOutput, calls=%fused_computation | convolution fusion | flops 807403520 | bytes 5373952 | tf_op jit(solution)/shard_map/dot_general | solution.py:25
  70.9 2.3 %token_grads.1 = bf16[6,196,1024]{2,1,0:T(8,128)(2,1)} custom-call(f32[6,16,196]{2,1,0:T(8,128)S(1)} %get-tuple-element.18.disp, bf16[6,16,196]{2,1,0:T(8,128)(2,1)S(1)} %get-tuple-element.24.lgrad, bf16[6,16,1024]{2,1,0:T(8,128)(2,1)S(1)} %get-tuple-element.25.sgrad, bf16[16,1024]{1,0:T(8,128)(2,1)S(1)} %get-tuple-element.26.router), custom_call_target="tpu_custom_call" | custom-call | flops 77070336 | bytes 2408448 | tf_op jit(solution)/shard_map/token_grads/pallas_call | solution.py:333
  73.1 0.0 collective-permute-done.8
  73.2 0.0 collective-permute-done.7
  73.2 0.0 collective-permute-done.6
  73.2 0.7 add_bitcast_fusion
  (3 shorter events, 0.1 us)
Async XLA Ops:
  25.9 1.7 %collective-permute-start = (bf16[384,512]{1,0:T(8,128)(2,1)S(1)}, bf16[384,512]{1,0:T(8,128)(2,1)S(1)}, u32[]{:S(2)}, u32[]{:S(2)}) collective-permute-start(bf16[384,512]{1,0:T(8,128)(2,1)S(1)} %bitcast.19), channel_id=1, source_target_pairs={{0,1},{1,0},{2,3},{3,2},{4,5},{5,4},{6,7},{7,6},{8,9},{9,8},{10,11... | collective-permute-start | bytes 1179656 | tf_op jit(solution)/shard_map/ppermute | solution.py:366
  27.7 24.4 %copy-start = (bf16[6,196,1024]{2,1,0:T(8,128)(2,1)S(1)}, bf16[6,196,1024]{2,1,0:T(8,128)(2,1)}, u32[]{:S(2)}) copy-start(bf16[6,196,1024]{2,1,0:T(8,128)(2,1)} %cot.1) | copy-start | bytes 7225348
  33.6 1.8 %collective-permute-start.1 = (bf16[192,1024]{1,0:T(8,128)(2,1)S(1)}, bf16[192,1024]{1,0:T(8,128)(2,1)S(1)}, u32[]{:S(2)}, u32[]{:S(2)}) collective-permute-start(bf16[192,1024]{1,0:T(8,128)(2,1)S(1)} %get-tuple-element.22), channel_id=1, source_target_pairs={{0,1},{1,0},{2,3},{3,2},{4,5},{5,4},{6,7},{7,6},{8,9},{9,8},{10,11... | collective-permute-start | bytes 1179656 | tf_op jit(solution)/shard_map/ppermute | solution.py:366
  54.9 1.3 %collective-permute-start.2 = (bf16[16,1024]{1,0:T(8,128)(2,1)S(1)}, bf16[16,1024]{1,0:T(8,128)(2,1)S(1)}, u32[]{:S(2)}, u32[]{:S(2)}) collective-permute-start(bf16[16,1024]{1,0:T(8,128)(2,1)S(1)} %reduce-precision_convert_fusion), channel_id=1, source_target_pairs={{0,1},{1,0},{2,3},{3,2},{4,5},{5,4},{6,7},{7,6},{8,9},{9,8},{10,11... | collective-permute-start | bytes 98312 | tf_op jit(solution)/shard_map/ppermute | solution.py:345
  56.2 6.9 %collective-permute-start.5 = (bf16[16,1024]{1,0:T(8,128)(2,1)S(1)}, bf16[16,1024]{1,0:T(8,128)(2,1)S(1)}, u32[]{:S(2)}, u32[]{:S(2)}) collective-permute-start(bf16[16,1024]{1,0:T(8,128)(2,1)S(1)} %fusion), channel_id=1, source_target_pairs={{0,6},{2,4},{4,2},{6,0},{8,14},{10,12},{12,10},{14,8},{16,22},{18,... | collective-permute-start | bytes 98312 | tf_op jit(solution)/shard_map/ppermute | solution.py:345
  57.1 6.0 %collective-permute-start.4 = (bf16[16,1024]{1,0:T(8,128)(2,1)S(1)}, bf16[16,1024]{1,0:T(8,128)(2,1)S(1)}, u32[]{:S(2)}, u32[]{:S(2)}) collective-permute-start(bf16[16,1024]{1,0:T(8,128)(2,1)S(1)} %fusion), channel_id=1, source_target_pairs={{0,4},{2,6},{4,0},{6,2},{8,12},{10,14},{12,8},{14,10},{16,20},{18,... | collective-permute-start | bytes 98312 | tf_op jit(solution)/shard_map/ppermute | solution.py:345
  58.3 4.8 %collective-permute-start.3 = (bf16[16,1024]{1,0:T(8,128)(2,1)S(1)}, bf16[16,1024]{1,0:T(8,128)(2,1)S(1)}, u32[]{:S(2)}, u32[]{:S(2)}) collective-permute-start(bf16[16,1024]{1,0:T(8,128)(2,1)S(1)} %fusion), channel_id=1, source_target_pairs={{0,2},{2,0},{4,6},{6,4},{8,10},{10,8},{12,14},{14,12},{16,18},{18,... | collective-permute-start | bytes 98312 | tf_op jit(solution)/shard_map/ppermute | solution.py:345
  63.1 10.1 %collective-permute-start.8 = (bf16[16,1024]{1,0:T(8,128)(2,1)S(1)}, bf16[16,1024]{1,0:T(8,128)(2,1)S(1)}, u32[]{:S(2)}, u32[]{:S(2)}) collective-permute-start(bf16[16,1024]{1,0:T(8,128)(2,1)S(1)} %fusion.1), channel_id=1, source_target_pairs={{0,24},{2,26},{4,28},{6,30},{8,16},{10,18},{12,20},{14,22},{16,8},... | collective-permute-start | bytes 98312 | tf_op jit(solution)/shard_map/ppermute | solution.py:345
  64.7 8.4 %collective-permute-start.7 = (bf16[16,1024]{1,0:T(8,128)(2,1)S(1)}, bf16[16,1024]{1,0:T(8,128)(2,1)S(1)}, u32[]{:S(2)}, u32[]{:S(2)}) collective-permute-start(bf16[16,1024]{1,0:T(8,128)(2,1)S(1)} %fusion.1), channel_id=1, source_target_pairs={{0,16},{2,18},{4,20},{6,22},{8,24},{10,26},{12,28},{14,30},{16,0},... | collective-permute-start | bytes 98312 | tf_op jit(solution)/shard_map/ppermute | solution.py:345
  65.7 7.5 %collective-permute-start.6 = (bf16[16,1024]{1,0:T(8,128)(2,1)S(1)}, bf16[16,1024]{1,0:T(8,128)(2,1)S(1)}, u32[]{:S(2)}, u32[]{:S(2)}) collective-permute-start(bf16[16,1024]{1,0:T(8,128)(2,1)S(1)} %fusion.1), channel_id=1, source_target_pairs={{0,8},{2,10},{4,12},{6,14},{8,0},{10,2},{12,4},{14,6},{16,24},{18,... | collective-permute-start | bytes 98312 | tf_op jit(solution)/shard_map/ppermute | solution.py:345

commit v2 on v1

--- a/solution.py
+++ b/solution.py
@@ -80,8 +80,8 @@
 
 def slots_kernel(
     pieces, chunk, tok_hbm, cot_hbm, router_hbm, weight,
-    send, disp, comb, router, held,
-    tok, cot, rows, tok_sems, cot_sems, router_sem, held_sems,
+    send, disp, comb, router, held, tok, cot,
+    rows, tok_sems, cot_sems, router_sem, held_sems,
 ):
     images, _, width = tok_hbm.shape
     experts = router_hbm.shape[0]
@@ -89,13 +89,12 @@
     router_copy.start()
     start_parts((tok_hbm, tok, tok_sems))
     start_parts((cot_hbm, cot, cot_sems))
+    start_parts((weight, held, held_sems))
     router_copy.wait()
     mixes = []
     for start in range(0, images, chunk):
         some = range(start, min(start + chunk, images))
         wait_parts(tok_hbm, tok, tok_sems, some)
-        if start + chunk >= images:
-            start_parts((weight, held, held_sems))
         logits = [mm(router[...], tok[n], 1, 1) for n in some]
         down = [jnp.exp(x - jnp.max(x, axis=1, keepdims=True)) for x in logits]
         across = [jnp.exp(x - jnp.max(x, axis=0, keepdims=True)) for x in logits]
@@ -131,12 +130,12 @@
             pltpu.VMEM((images, experts, toks), F32),
             pltpu.VMEM(router_t.shape, BF),
             pltpu.VMEM(weight.shape, BF),
+            pltpu.VMEM(tokens.shape, BF),
+            pltpu.VMEM(tokens.shape, BF),
         ),
         in_specs=[HBM] * 4,
-        out_specs=(VM,) * 5,
+        out_specs=(VM,) * 7,
         scratch_shapes=[
-            pltpu.VMEM(tokens.shape, BF),
-            pltpu.VMEM(tokens.shape, BF),
             pltpu.VMEM((2 * images * experts, width), BF),
             pltpu.SemaphoreType.DMA((images,)),
             pltpu.SemaphoreType.DMA((images,)),
@@ -149,10 +148,27 @@
     )(*(in_hbm(x) for x in (tokens, out_grad, router_t, weight)))
 
 
+def fetch_kernel(source, target, sems):
+    start_parts((source, target, sems))
+    wait_parts(source, target, sems)
+
+
+def fetch(weight):
+    return pl.pallas_call(
+        fetch_kernel,
+        out_shape=pltpu.VMEM(weight.shape, BF),
+        in_specs=[HBM],
+        out_specs=VM,
+        scratch_shapes=[pltpu.SemaphoreType.DMA((8,))],
+        compiler_params=params(8),
+        cost_estimate=cost(0, 2 * weight.size),
+        name="fetch",
+    )(in_hbm(weight))
+
+
 def expert_kernel(
-    pieces, images, mine, theirs, w_in, w_out_hbm, keep, give, slot, cot, act, hgrad, slope, w_out, sems
+    pieces, images, mine, theirs, w_in, w_out, keep, give, slot, cot, act, hgrad
 ):
-    start_parts((w_out_hbm, w_out, sems))
     half = mine.shape[0] // (2 * pieces)
     part = mine.shape[1]
     width = pieces * part
@@ -180,14 +196,12 @@
     step = 256
     for f in range(0, hidden, step):
         x = mm(slot[...], w_in[:, f : f + step])
+        g = mm(cot[...], w_out[f : f + step, :], 1, 1)
         inner = x * (ROOT * CUBE * (x * x) + ROOT)
         up = 0.5 * jnp.tanh(inner) + 0.5
         act[:, f : f + step] = (x * up).astype(BF)
-        slope[:, f : f + step] = up + up * (1.0 - up) * (6.0 * inner - 4.0 * ROOT * x)
-    wait_parts(w_out_hbm, w_out, sems)
-    for f in range(0, hidden, step):
-        g = mm(cot[...], w_out[f : f + step, :], 1, 1)
-        hgrad[:, f : f + step] = (g * slope[:, f : f + step]).astype(BF)
+        slope = up + up * (1.0 - up) * (6.0 * inner - 4.0 * ROOT * x)
+        hgrad[:, f : f + step] = (g * slope).astype(BF)
     step = 256
     for c in range(0, width, step):
         columns = slice(c, c + step)
@@ -214,17 +228,12 @@
             jax.ShapeDtypeStruct((rows, hidden), BF),
             jax.ShapeDtypeStruct((rows, hidden), BF),
         ),
-        in_specs=[VM, VM, VM, HBM],
+        in_specs=[VM] * 4,
         out_specs=(VM,) * 6,
-        scratch_shapes=[
-            pltpu.VMEM((rows, hidden), F32),
-            pltpu.VMEM(w_out.shape, BF),
-            pltpu.SemaphoreType.DMA((8,)),
-        ],
         compiler_params=params(32),
         cost_estimate=cost(8 * rows * width * hidden, 4 * width * hidden),
         name="expert",
-    )(mine, theirs, w_in, in_hbm(w_out))
+    )(mine, theirs, w_in, w_out)
 
 
 def join_kernel(pieces, images, keep, got, send):
@@ -258,7 +267,7 @@
     rows, width = keep.shape
     return pl.pallas_call(
         functools.partial(join_kernel, pieces, images),
-        out_shape=jax.ShapeDtypeStruct((rows * pieces, width // pieces), BF),
+        out_shape=pltpu.VMEM((rows * pieces, width // pieces), BF),
         in_specs=[VM] * 2,
         out_specs=VM,
         compiler_params=params(8),
@@ -268,10 +277,9 @@
 
 
 def logits_kernel(
-    pieces, back, tok_hbm, cot, disp, comb, part_out, lgrad, sgrad, tok, rows, sems
+    pieces, back, tok, cot, disp, comb, part_out, lgrad, sgrad, rows
 ):
     images, experts, _ = disp.shape
-    start_parts((tok_hbm, tok, sems))
     kind = 2 * images
     part = back.shape[1]
     for count in range(pieces):
@@ -282,7 +290,6 @@
     every = range(images)
     c = [mm(rows[n * experts : (n + 1) * experts, :], cot[n], 1, 1) for n in every]
     c = [comb[n] * (x - jnp.sum(comb[n] * x, axis=0, keepdims=True)) for n, x in zip(every, c)]
-    wait_parts(tok_hbm, tok, sems)
     slots = [rows[(images + n) * experts : (images + n + 1) * experts, :] for n in every]
     d = [mm(x, tok[n], 1, 1) for n, x in zip(every, slots)]
     d = [disp[n] * (x - jnp.sum(disp[n] * x, axis=1, keepdims=True)) for n, x in zip(every, d)]
@@ -307,17 +314,43 @@
             jax.ShapeDtypeStruct((images, experts, toks), BF),
             jax.ShapeDtypeStruct((images, experts, width), BF),
         ),
-        in_specs=[VM, HBM, VM, VM, VM],
+        in_specs=[VM] * 5,
         out_specs=(VM,) * 3,
-        scratch_shapes=[
-            pltpu.VMEM(tok.shape, BF),
-            pltpu.VMEM((2 * images * experts, width), BF),
-            pltpu.SemaphoreType.DMA((images,)),
-        ],
+        scratch_shapes=[pltpu.VMEM((2 * images * experts, width), BF)],
         compiler_params=params(16),
         cost_estimate=cost(6 * images * toks * width * experts, 4 * images * toks * width),
         name="logit_grads",
-    )(back, in_hbm(tok), cot, disp, comb)
+    )(back, tok, cot, disp, comb)
+
+
+def weight_kernel(left, right, out, held, sems):
+    parts = sems.shape[0]
+    size = out.shape[0] // parts
+    for i in range(parts):
+        rows = pl.ds(i * size, size)
+        held[rows, :] = mm(left[:, i * size : (i + 1) * size], right[...], 0, 0).astype(BF)
+
+        @pl.when(pl.program_id(0) >= 0)
+        def _():
+            pltpu.make_async_copy(held.at[rows], out.at[rows], sems.at[i]).start()
+
+    for i in range(parts):
+        rows = pl.ds(i * size, size)
+        pltpu.make_async_copy(held.at[rows], out.at[rows], sems.at[i]).wait()
+
+
+def weight_grad(left, right):
+    shape = (left.shape[1], right.shape[1])
+    return pl.pallas_call(
+        weight_kernel,
+        grid=(1,),
+        out_shape=jax.ShapeDtypeStruct(shape, BF),
+        in_specs=[VM] * 2,
+        out_specs=HBM,
+        scratch_shapes=[pltpu.VMEM(shape, BF), pltpu.SemaphoreType.DMA((8,))],
+        compiler_params=params(16),
+        cost_estimate=cost(2 * left.size * right.shape[1], 2 * shape[0] * shape[1]),
+    )(left, right)
 
 
 def tokens_kernel(disp, lgrad, sgrad, router, out):
@@ -341,50 +374,61 @@
     )(disp, lgrad, sgrad, router_t)
 
 
-def xor_permute(x, axis, size, mask):
-    return lax.ppermute(x, axis, [(i, i ^ mask) for i in range(size)])
-
-
-def all_sum(x, sizes):
-    for axis in ("pair", "expert"):
-        size, step = sizes[axis], 1
-        while step < size:
-            span = 4 if size // step >= 4 else 2
-            x = lax.reduce_precision(x, 8, 7)
-            sent = x.astype(BF)
-            got = [xor_permute(sent, axis, size, step * k) for k in range(1, span)]
-            got = [x] + [part.astype(F32) for part in got]
-            x = got[0] + got[1]
-            if span == 4:
-                x = x + (got[2] + got[3])
-            step *= span
+def rounded(x):
+    return lax.reduce_precision(x, 8, 7)
+
+
+def swap_pair(x):
+    return lax.ppermute(x, "pair", [(0, 1), (1, 0)])
+
+
+def toward(x, size, mask):
+    return lax.ppermute(x, "expert", [(i, i ^ mask) for i in range(size)]).astype(F32)
+
+
+def all_sum(x, size):
+    x = rounded(x)
+    x = x + swap_pair(x.astype(BF)).astype(F32)
+    step = 1
+    while step < size:
+        x = rounded(x)
+        sent = x.astype(BF)
+        got = toward(sent, size, step)
+        x = x + got
+        if size // step >= 4:
+            got = toward(sent, size, 2 * step)
+            got = got + toward(sent, size, 3 * step)
+            x = x + got
+            step *= 4
+        else:
+            step *= 2
     return x
 
 
 def make_per_device(sizes):
-    def swap(x):
-        return lax.ppermute(x, "pair", [(0, 1), (1, 0)])
-
     def exchange(x):
         blocks = x.reshape(sizes["expert"], -1, x.shape[1])
         return lax.all_to_all(blocks, "expert", split_axis=0, concat_axis=0, tiled=True).reshape(x.shape)
 
     def per_device(tokens, router, w_in, w_out, out_grad):
         images = tokens.shape[0]
-        send, disp, comb, router_t, held_in = make_slots(tokens, out_grad, router.T, w_in[0])
+        send, disp, comb, router_t, held_in, tok, cot = make_slots(
+            tokens, out_grad, router.T, w_in[0]
+        )
         mine = exchange(send)
-        theirs = swap(mine)
+        theirs = swap_pair(mine)
+        held_out = fetch(w_out[0])
         keep, give, slot_rows, cot_rows, act, hgrad = run_expert(
-            mine, theirs, held_in, w_out[0], images
+            mine, theirs, held_in, held_out, images
         )
-        got = swap(give)
+        got = swap_pair(give)
         joined = join(keep, got, images)
         back = exchange(joined)
-        grad_in = mm(slot_rows, hgrad, 0, 0).astype(BF)
-        grad_out = mm(act, cot_rows, 0, 0).astype(BF)
-        part, lgrad, sgrad = logit_grads(back, tokens, out_grad, disp, comb)
+        grad_in = weight_grad(slot_rows, hgrad)
+        grad_out = weight_grad(act, cot_rows)
+        part, lgrad, sgrad = logit_grads(back, tok, cot, disp, comb)
         tokens_grad = token_grads(disp, lgrad, sgrad, router_t)
-        router_grad = all_sum(part, sizes).T
+        router_grad = all_sum(part, sizes["expert"]).T
         return tokens_grad, grad_in[None], grad_out[None], router_grad
 
     return per_device

time: 74.1 us -> 70.4 us (0.950)
  matrix products: 6.63 us -> 0 us
  Pallas kernels: 15.9 us -> 20.2 us
  waiting for transfers between devices: 4.51 us -> 2.59 us
    pallas_call x0 -> x3, Pallas kernels: none -> 7 us  [the longest x2 4.79 us: weight_grad(): pl.pallas_call(weight_kernel, grid=(1,), out_shape=jax.ShapeDtypeStruct(s...]
    dot_general x2 -> x0, matrix products: 6.63 us -> none  [mm(): lax.dot_general(a, b, (((da,), (db,)), ((), ())), preferred_element_type=...]
    ppermute x9, waiting for transfers between devices: 4.51 us -> 2.59 us  [the longest x3 2.55 us: swap_pair(): return lax.ppermute(x, 'pair', [(0, 1), (1, 0)])]
    pallas_call x1, Pallas kernels: 5.92 us -> 4.53 us  [run_expert(): pl.pallas_call(functools.partial(expert_kernel, pieces, images), out_shap...]
    pallas_call x1, Pallas kernels: 2.8 us -> 1.97 us  [logit_grads(): pl.pallas_call(functools.partial(logits_kernel, pieces), out_shape=(jax.S...]
  transfers between devices with their start and end apart: 9 -> 9, of which waited for: 3 -> 2; matrix products, arithmetic and copies ran while one was open for 9% -> 0% of each run, Pallas kernels for 3% -> 13%
where the time goes in v2:
time: 70.4 us; the launch traced here: 70.2 us
  blocking collectives  37.3 us (53%)
  Pallas kernels  20.2 us (29%)
  starting transfers between devices  8.66 us (12%)
  waiting for transfers between devices  2.59 us (4%)
  between operations  0.73 us (1%)
  other arithmetic  0.72 us (1%)
    all_to_all x2, blocking collectives, exchange(): lax.all_to_all(blocks, 'expert', split_axis=0, concat_axis=0, tiled=True)  37.3 us
    ppermute x6, starting transfers between devices, toward(): lax.ppermute(x, 'expert', [(i, i ^ mask) for i in range(size)]).astype(F32)  8.01 us
    pallas_call x2, Pallas kernels, weight_grad(): pl.pallas_call(weight_kernel, grid=(1,), out_shape=jax.ShapeDtypeStruct(s...  4.79 us
    pallas_call x1, Pallas kernels, run_expert(): pl.pallas_call(functools.partial(expert_kernel, pieces, images), out_shap...  4.53 us
    pallas_call x1, Pallas kernels, make_slots(): pl.pallas_call(functools.partial(slots_kernel, pieces, 3), out_shape=(plt...  4.01 us
    ppermute x3, waiting for transfers between devices, swap_pair(): return lax.ppermute(x, 'pair', [(0, 1), (1, 0)])  2.55 us
    pallas_call x1, Pallas kernels, token_grads(): pl.pallas_call(tokens_kernel, out_shape=jax.ShapeDtypeStruct((images, tok...  2.28 us
    pallas_call x1, Pallas kernels, fetch(): pl.pallas_call(fetch_kernel, out_shape=pltpu.VMEM(weight.shape, BF), in_s...  2.21 us
  transfers between devices with their start and end apart: 9, of which 2 were waited for; matrix products, arithmetic and copies ran while one was open for 0% of the time, Pallas kernels for 13%

profile of v2, /device:TPU:0, one launch (start us, length us, event | category | flops | bytes accessed | tf_op | source)
XLA Modules:
  0.0 70.2 jit_solution(14335844885399751916)
XLA Ops:
  0.6 4.0 %slots.1 = (bf16[384,512]{1,0:T(8,128)(2,1)S(1)}, f32[6,16,196]{2,1,0:T(8,128)S(1)}, f32[6,16,196]{2,1,0:T(8,128)S(1)}, bf16[16,1024]{1,0:T(8,128)(2,1)S(1)}, bf...) custom-call(bf16[6,196,1024]{2,1,0:T(8,128)(2,1)} %tok_hbm.1, ...), custom_call_target="tpu_custom_call" | custom-call | flops 115605504 | bytes 4816896 | tf_op jit(solution)/shard_map/slots/pallas_call | solution.py:125
  4.7 20.8 %all_to_all.10 = bf16[16,24,512]{2,1,0:T(8,128)(2,1)S(1)} all-to-all(bf16[16,24,512]{2,1,0:T(8,128)(2,1)S(1)} %bitcast.15), channel_id=1, replica_groups=mesh['expert'=16,'pair'=2] {'expert'}, dimensions={0} | all-to-all | bytes 786432 | tf_op jit(solution)/shard_map/all_to_all | solution.py:411
  25.4 0.0 collective-permute-start
  25.4 2.2 %fetch.1.w_out = bf16[2048,1024]{1,0:T(8,128)(2,1)S(1)} custom-call(bf16[2048,1024]{1,0:T(8,128)(2,1)} %bitcast.17), custom_call_target="tpu_custom_call" | custom-call | bytes 4194304 | tf_op jit(solution)/shard_map/fetch/pallas_call | solution.py:157
  27.6 0.0 collective-permute-done.theirs
  27.7 4.5 %expert.1 = (f32[192,1024]{1,0:T(8,128)S(1)}, bf16[192,1024]{1,0:T(8,128)(2,1)S(1)}, bf16[192,1024]{1,0:T(8,128)(2,1)S(1)}, bf16[192,1024]{1,0:T(8,128)(2,1)S(1)...) custom-call(bf16[384,512]{1,0:T(8,128)(2,1)S(1)} %bitcast.14, ...), custom_call_target="tpu_custom_call" | custom-call | flops 3221225472 | bytes 8388608 | tf_op jit(solution)/shard_map/expert/pallas_call | solution.py:221
  32.2 0.6 collective-permute-start.1
  32.8 1.3 %collective-permute-done.1.got = bf16[192,1024]{1,0:T(8,128)(2,1)S(1)} collective-permute-done((bf16[192,1024]{1,0:T(8,128)(2,1)S(1)}, bf16[192,1024]{1,0:T(8,128)(2,1)S(1)}, u32[]{:S(2)}, u32[]{:S(2)}) %collective-permute-start.1) | collective-permute-done | bytes 393248 | tf_op jit(solution)/shard_map/ppermute | solution.py:382
  34.1 0.4 join.1
  34.5 16.5 %all_to_all.11 = bf16[16,24,512]{2,1,0:T(8,128)(2,1)S(1)} all-to-all(bf16[16,24,512]{2,1,0:T(8,128)(2,1)S(1)} %bitcast.11), channel_id=1, replica_groups=mesh['expert'=16,'pair'=2] {'expert'}, dimensions={0} | all-to-all | bytes 786432 | tf_op jit(solution)/shard_map/all_to_all | solution.py:411
  51.0 2.0 %logit_grads.1 = (f32[16,1024]{1,0:T(8,128)S(1)}, bf16[6,16,196]{2,1,0:T(8,128)(2,1)S(1)}, bf16[6,16,1024]{2,1,0:T(8,128)(2,1)S(1)}) custom-call(bf16[384,512]{1,0:T(8,128)(2,1)S(1)} %bitcast.12, bf16[6,196,1024]{2,1,0:T(8,128)(2,1)S(1)} %get-tuple-element.25.tok, bf16[6,196,1024]{2,1,0:T(8,128)(2,1)S(1)} %get-tuple-element.26.cot, ...), custom_call_target="tpu_custom_call" | custom-call | flops 115605504 | bytes 4816896 | tf_op jit(solution)/shard_map/logit_grads/pallas_call | solution.py:310
  53.0 0.1 collective-permute-start.2
  53.1 1.2 %collective-permute-done.2 = bf16[16,1024]{1,0:T(8,128)(2,1)S(1)} collective-permute-done((bf16[16,1024]{1,0:T(8,128)(2,1)S(1)}, bf16[16,1024]{1,0:T(8,128)(2,1)S(1)}, u32[]{:S(2)}, u32[]{:S(2)}) %collective-permute-start.2) | collective-permute-done | bytes 32800 | tf_op jit(solution)/shard_map/ppermute | solution.py:382
  54.3 0.9 %collective-permute-start.5 = (bf16[16,1024]{1,0:T(8,128)(2,1)S(1)}, bf16[16,1024]{1,0:T(8,128)(2,1)S(1)}, u32[]{:S(2)}, u32[]{:S(2)}) collective-permute-start(bf16[16,1024]{1,0:T(8,128)(2,1)S(1)} %fusion), channel_id=1, source_target_pairs={{0,6},{2,4},{4,2},{6,0},{8,14},{10,12},{12,10},{14,8},{16,22},{18,... | collective-permute-start | bytes 98312 | tf_op jit(solution)/shard_map/ppermute | solution.py:386
  55.2 1.2 %collective-permute-start.4 = (bf16[16,1024]{1,0:T(8,128)(2,1)S(1)}, bf16[16,1024]{1,0:T(8,128)(2,1)S(1)}, u32[]{:S(2)}, u32[]{:S(2)}) collective-permute-start(bf16[16,1024]{1,0:T(8,128)(2,1)S(1)} %fusion), channel_id=1, source_target_pairs={{0,4},{2,6},{4,0},{6,2},{8,12},{10,14},{12,8},{14,10},{16,20},{18,... | collective-permute-start | bytes 98312 | tf_op jit(solution)/shard_map/ppermute | solution.py:386
  56.4 1.5 %collective-permute-start.3 = (bf16[16,1024]{1,0:T(8,128)(2,1)S(1)}, bf16[16,1024]{1,0:T(8,128)(2,1)S(1)}, u32[]{:S(2)}, u32[]{:S(2)}) collective-permute-start(bf16[16,1024]{1,0:T(8,128)(2,1)S(1)} %fusion), channel_id=1, source_target_pairs={{0,2},{2,0},{4,6},{6,4},{8,10},{10,8},{12,14},{14,12},{16,18},{18,... | collective-permute-start | bytes 98312 | tf_op jit(solution)/shard_map/ppermute | solution.py:386
  57.9 2.4 %shard_map.84 = bf16[1024,2048]{1,0:T(8,128)(2,1)} custom-call(bf16[192,1024]{1,0:T(8,128)(2,1)S(1)} %get-tuple-element.31.left, bf16[192,2048]{1,0:T(8,128)(2,1)S(1)} %get-tuple-element.32.right), custom_call_target="tpu_custom_call" | custom-call | flops 805306368 | bytes 4194304 | tf_op jit(solution)/shard_map/pallas_call | solution.py:344
  60.3 0.0 collective-permute-done.5
  60.3 0.0 collective-permute-done.4
  60.3 0.0 collective-permute-done.3
  60.3 1.6 %collective-permute-start.8 = (bf16[16,1024]{1,0:T(8,128)(2,1)S(1)}, bf16[16,1024]{1,0:T(8,128)(2,1)S(1)}, u32[]{:S(2)}, u32[]{:S(2)}) collective-permute-start(bf16[16,1024]{1,0:T(8,128)(2,1)S(1)} %fusion.1), channel_id=1, source_target_pairs={{0,24},{2,26},{4,28},{6,30},{8,16},{10,18},{12,20},{14,22},{16,8},... | collective-permute-start | bytes 98312 | tf_op jit(solution)/shard_map/ppermute | solution.py:386
  62.0 1.0 %collective-permute-start.7 = (bf16[16,1024]{1,0:T(8,128)(2,1)S(1)}, bf16[16,1024]{1,0:T(8,128)(2,1)S(1)}, u32[]{:S(2)}, u32[]{:S(2)}) collective-permute-start(bf16[16,1024]{1,0:T(8,128)(2,1)S(1)} %fusion.1), channel_id=1, source_target_pairs={{0,16},{2,18},{4,20},{6,22},{8,24},{10,26},{12,28},{14,30},{16,0},... | collective-permute-start | bytes 98312 | tf_op jit(solution)/shard_map/ppermute | solution.py:386
  63.0 1.8 %collective-permute-start.6 = (bf16[16,1024]{1,0:T(8,128)(2,1)S(1)}, bf16[16,1024]{1,0:T(8,128)(2,1)S(1)}, u32[]{:S(2)}, u32[]{:S(2)}) collective-permute-start(bf16[16,1024]{1,0:T(8,128)(2,1)S(1)} %fusion.1), channel_id=1, source_target_pairs={{0,8},{2,10},{4,12},{6,14},{8,0},{10,2},{12,4},{14,6},{16,24},{18,... | collective-permute-start | bytes 98312 | tf_op jit(solution)/shard_map/ppermute | solution.py:386
  64.8 2.4 %shard_map.85 = bf16[2048,1024]{1,0:T(8,128)(2,1)} custom-call(bf16[192,2048]{1,0:T(8,128)(2,1)S(1)} %get-tuple-element.33.left, bf16[192,1024]{1,0:T(8,128)(2,1)S(1)} %get-tuple-element.34.right), custom_call_target="tpu_custom_call" | custom-call | flops 805306368 | bytes 4194304 | tf_op jit(solution)/shard_map/pallas_call | solution.py:344
  67.2 2.3 %token_grads.1 = bf16[6,196,1024]{2,1,0:T(8,128)(2,1)} custom-call(f32[6,16,196]{2,1,0:T(8,128)S(1)} %get-tuple-element.20.disp, bf16[6,16,196]{2,1,0:T(8,128)(2,1)S(1)} %get-tuple-element.28.lgrad, bf16[6,16,1024]{2,1,0:T(8,128)(2,1)S(1)} %get-tuple-element.29.sgrad, bf16[16,1024]{1,0:T(8,128)(2,1)S(1)} %get-tuple-element.30.router), custom_call_target="tpu_custom_call" | custom-call | flops 77070336 | bytes 2408448 | tf_op jit(solution)/shard_map/token_grads/pallas_call | solution.py:366
  69.5 0.0 collective-permute-done.8
  69.5 0.0 collective-permute-done.7
  69.5 0.0 collective-permute-done.6
  69.5 0.7 add_bitcast_fusion
  (3 shorter events, 0.0 us)
Async XLA Ops:
  25.4 2.2 %collective-permute-start = (bf16[384,512]{1,0:T(8,128)(2,1)S(1)}, bf16[384,512]{1,0:T(8,128)(2,1)S(1)}, u32[]{:S(2)}, u32[]{:S(2)}) collective-permute-start(bf16[384,512]{1,0:T(8,128)(2,1)S(1)} %bitcast.13), channel_id=1, source_target_pairs={{0,1},{1,0},{2,3},{3,2},{4,5},{5,4},{6,7},{7,6},{8,9},{9,8},{10,11... | collective-permute-start | bytes 1179656 | tf_op jit(solution)/shard_map/ppermute | solution.py:382
  32.2 1.9 %collective-permute-start.1 = (bf16[192,1024]{1,0:T(8,128)(2,1)S(1)}, bf16[192,1024]{1,0:T(8,128)(2,1)S(1)}, u32[]{:S(2)}, u32[]{:S(2)}) collective-permute-start(bf16[192,1024]{1,0:T(8,128)(2,1)S(1)} %get-tuple-element.24), channel_id=1, source_target_pairs={{0,1},{1,0},{2,3},{3,2},{4,5},{5,4},{6,7},{7,6},{8,9},{9,8},{10,11... | collective-permute-start | bytes 1179656 | tf_op jit(solution)/shard_map/ppermute | solution.py:382
  53.0 1.3 %collective-permute-start.2 = (bf16[16,1024]{1,0:T(8,128)(2,1)S(1)}, bf16[16,1024]{1,0:T(8,128)(2,1)S(1)}, u32[]{:S(2)}, u32[]{:S(2)}) collective-permute-start(bf16[16,1024]{1,0:T(8,128)(2,1)S(1)} %reduce-precision_convert_fusion), channel_id=1, source_target_pairs={{0,1},{1,0},{2,3},{3,2},{4,5},{5,4},{6,7},{7,6},{8,9},{9,8},{10,11... | collective-permute-start | bytes 98312 | tf_op jit(solution)/shard_map/ppermute | solution.py:382
  54.3 6.0 %collective-permute-start.5 = (bf16[16,1024]{1,0:T(8,128)(2,1)S(1)}, bf16[16,1024]{1,0:T(8,128)(2,1)S(1)}, u32[]{:S(2)}, u32[]{:S(2)}) collective-permute-start(bf16[16,1024]{1,0:T(8,128)(2,1)S(1)} %fusion), channel_id=1, source_target_pairs={{0,6},{2,4},{4,2},{6,0},{8,14},{10,12},{12,10},{14,8},{16,22},{18,... | collective-permute-start | bytes 98312 | tf_op jit(solution)/shard_map/ppermute | solution.py:386
  55.2 5.1 %collective-permute-start.4 = (bf16[16,1024]{1,0:T(8,128)(2,1)S(1)}, bf16[16,1024]{1,0:T(8,128)(2,1)S(1)}, u32[]{:S(2)}, u32[]{:S(2)}) collective-permute-start(bf16[16,1024]{1,0:T(8,128)(2,1)S(1)} %fusion), channel_id=1, source_target_pairs={{0,4},{2,6},{4,0},{6,2},{8,12},{10,14},{12,8},{14,10},{16,20},{18,... | collective-permute-start | bytes 98312 | tf_op jit(solution)/shard_map/ppermute | solution.py:386
  56.4 3.9 %collective-permute-start.3 = (bf16[16,1024]{1,0:T(8,128)(2,1)S(1)}, bf16[16,1024]{1,0:T(8,128)(2,1)S(1)}, u32[]{:S(2)}, u32[]{:S(2)}) collective-permute-start(bf16[16,1024]{1,0:T(8,128)(2,1)S(1)} %fusion), channel_id=1, source_target_pairs={{0,2},{2,0},{4,6},{6,4},{8,10},{10,8},{12,14},{14,12},{16,18},{18,... | collective-permute-start | bytes 98312 | tf_op jit(solution)/shard_map/ppermute | solution.py:386
  60.3 9.1 %collective-permute-start.8 = (bf16[16,1024]{1,0:T(8,128)(2,1)S(1)}, bf16[16,1024]{1,0:T(8,128)(2,1)S(1)}, u32[]{:S(2)}, u32[]{:S(2)}) collective-permute-start(bf16[16,1024]{1,0:T(8,128)(2,1)S(1)} %fusion.1), channel_id=1, source_target_pairs={{0,24},{2,26},{4,28},{6,30},{8,16},{10,18},{12,20},{14,22},{16,8},... | collective-permute-start | bytes 98312 | tf_op jit(solution)/shard_map/ppermute | solution.py:386
  62.0 7.5 %collective-permute-start.7 = (bf16[16,1024]{1,0:T(8,128)(2,1)S(1)}, bf16[16,1024]{1,0:T(8,128)(2,1)S(1)}, u32[]{:S(2)}, u32[]{:S(2)}) collective-permute-start(bf16[16,1024]{1,0:T(8,128)(2,1)S(1)} %fusion.1), channel_id=1, source_target_pairs={{0,16},{2,18},{4,20},{6,22},{8,24},{10,26},{12,28},{14,30},{16,0},... | collective-permute-start | bytes 98312 | tf_op jit(solution)/shard_map/ppermute | solution.py:386
  63.0 6.5 %collective-permute-start.6 = (bf16[16,1024]{1,0:T(8,128)(2,1)S(1)}, bf16[16,1024]{1,0:T(8,128)(2,1)S(1)}, u32[]{:S(2)}, u32[]{:S(2)}) collective-permute-start(bf16[16,1024]{1,0:T(8,128)(2,1)S(1)} %fusion.1), channel_id=1, source_target_pairs={{0,8},{2,10},{4,12},{6,14},{8,0},{10,2},{12,4},{14,6},{16,24},{18,... | collective-permute-start | bytes 98312 | tf_op jit(solution)/shard_map/ppermute | solution.py:386

commit v3 on v2

--- a/solution.py
+++ b/solution.py
@@ -148,35 +148,12 @@
     )(*(in_hbm(x) for x in (tokens, out_grad, router_t, weight)))
 
 
-def fetch_kernel(source, target, sems):
-    start_parts((source, target, sems))
-    wait_parts(source, target, sems)
-
-
-def fetch(weight):
-    return pl.pallas_call(
-        fetch_kernel,
-        out_shape=pltpu.VMEM(weight.shape, BF),
-        in_specs=[HBM],
-        out_specs=VM,
-        scratch_shapes=[pltpu.SemaphoreType.DMA((8,))],
-        compiler_params=params(8),
-        cost_estimate=cost(0, 2 * weight.size),
-        name="fetch",
-    )(in_hbm(weight))
-
-
-def expert_kernel(
-    pieces, images, mine, theirs, w_in, w_out, keep, give, slot, cot, act, hgrad
-):
-    half = mine.shape[0] // (2 * pieces)
-    part = mine.shape[1]
-    width = pieces * part
-    hidden = w_in.shape[1]
+def place_rows(pieces, images, block_rows, slot, cot, base):
+    part = block_rows.shape[1]
     kind = 2 * images
-    groups = mine.shape[0] // (pieces * kind)
+    block = pieces * kind
+    groups = block_rows.shape[0] // block
     some = math.gcd(groups, 8)
-    block = pieces * kind
     column = lax.broadcasted_iota(jnp.int32, (1, some * block), 1)
     source = column // block
     place = column - source * block
@@ -185,26 +162,73 @@
     row = lax.broadcasted_iota(jnp.int32, (some * block, some * block), 0)
     pick = jnp.where(row == wanted, 1.0, 0.0).astype(BF)
     size = some * images
-    for base, ref in ((0, mine), (half, theirs)):
-        for group in range(groups // some):
-            both = mm(pick, ref[group * some * block : (group + 1) * some * block, :]).astype(BF)
-            at = base + group * size
-            for count in range(pieces):
-                columns = slice(count * part, (count + 1) * part)
-                slot[at : at + size, columns] = both[2 * count * size : (2 * count + 1) * size]
-                cot[at : at + size, columns] = both[(2 * count + 1) * size : (2 * count + 2) * size]
-    step = 256
-    for f in range(0, hidden, step):
-        x = mm(slot[...], w_in[:, f : f + step])
-        g = mm(cot[...], w_out[f : f + step, :], 1, 1)
-        inner = x * (ROOT * CUBE * (x * x) + ROOT)
-        up = 0.5 * jnp.tanh(inner) + 0.5
-        act[:, f : f + step] = (x * up).astype(BF)
-        slope = up + up * (1.0 - up) * (6.0 * inner - 4.0 * ROOT * x)
-        hgrad[:, f : f + step] = (g * slope).astype(BF)
-    step = 256
-    for c in range(0, width, step):
-        columns = slice(c, c + step)
+    for group in range(groups // some):
+        both = mm(pick, block_rows[group * some * block : (group + 1) * some * block, :]).astype(BF)
+        at = base + group * size
+        for count in range(pieces):
+            columns = slice(count * part, (count + 1) * part)
+            slot[at : at + size, columns] = both[2 * count * size : (2 * count + 1) * size]
+            cot[at : at + size, columns] = both[(2 * count + 1) * size : (2 * count + 2) * size]
+
+
+def gelu_parts(x):
+    inner = x * (ROOT * CUBE * (x * x) + ROOT)
+    up = 0.5 * jnp.tanh(inner) + 0.5
+    return x * up, up + up * (1.0 - up) * (6.0 * inner - 4.0 * ROOT * x)
+
+
+STEP = 256
+
+
+def own_kernel(pieces, images, mine, w_in, w_out_hbm, w_out, slot, cot, act, slope, sems):
+    start_parts((w_out_hbm, w_out, sems))
+    half = slope.shape[0]
+    place_rows(pieces, images, mine, slot, cot, 0)
+    for f in range(0, w_in.shape[1], STEP):
+        value, rise = gelu_parts(mm(slot[:half, :], w_in[:, f : f + STEP]))
+        act[:half, f : f + STEP] = value.astype(BF)
+        slope[:, f : f + STEP] = rise
+    wait_parts(w_out_hbm, w_out, sems)
+
+
+def run_own(mine, w_in, w_out, images):
+    pieces = pieces_of(images)
+    rows = mine.shape[0] // pieces
+    width, hidden = w_in.shape
+    return pl.pallas_call(
+        functools.partial(own_kernel, pieces, images),
+        out_shape=(
+            pltpu.VMEM(w_out.shape, BF),
+            pltpu.VMEM((rows, width), BF),
+            pltpu.VMEM((rows, width), BF),
+            pltpu.VMEM((rows, hidden), BF),
+            pltpu.VMEM((rows // 2, hidden), F32),
+        ),
+        in_specs=[VM, VM, HBM],
+        out_specs=(VM,) * 5,
+        scratch_shapes=[pltpu.SemaphoreType.DMA((8,))],
+        compiler_params=params(16),
+        cost_estimate=cost(rows * width * hidden, 2 * w_out.size),
+        name="own",
+    )(mine, w_in, in_hbm(w_out))
+
+
+def expert_kernel(
+    pieces, images, theirs, w_in, w_out, slope, *refs
+):
+    keep, give, slot, cot, act, hgrad = refs[3:]
+    width, hidden = w_in.shape
+    half = slope.shape[0]
+    place_rows(pieces, images, theirs, slot, cot, half)
+    for f in range(0, hidden, STEP):
+        columns = slice(f, f + STEP)
+        value, rise = gelu_parts(mm(slot[half:, :], w_in[:, columns]))
+        act[half:, columns] = value.astype(BF)
+        g = mm(cot[...], w_out[columns, :], 1, 1)
+        hgrad[:half, columns] = (g[:half] * slope[:, columns]).astype(BF)
+        hgrad[half:, columns] = (g[half:] * rise).astype(BF)
+    for c in range(0, width, STEP):
+        columns = slice(c, c + STEP)
         value = mm(act[...], w_out[:, columns])
         keep[:half, columns] = value[:half]
         give[:half, columns] = value[half:].astype(BF)
@@ -213,27 +237,27 @@
         give[half:, columns] = value[half:].astype(BF)
 
 
-def run_expert(mine, theirs, w_in, w_out, images):
+def run_expert(theirs, w_in, w_out, slope, slot, cot, act, images):
     pieces = pieces_of(images)
-    rows = mine.shape[0] // pieces
-    width = w_in.shape[0]
-    hidden = w_in.shape[1]
+    rows, width = slot.shape
+    hidden = act.shape[1]
     return pl.pallas_call(
         functools.partial(expert_kernel, pieces, images),
         out_shape=(
             jax.ShapeDtypeStruct((rows, width), F32),
             jax.ShapeDtypeStruct((rows, width), BF),
-            jax.ShapeDtypeStruct((rows, width), BF),
-            jax.ShapeDtypeStruct((rows, width), BF),
-            jax.ShapeDtypeStruct((rows, hidden), BF),
+            pltpu.VMEM((rows, width), BF),
+            pltpu.VMEM((rows, width), BF),
+            pltpu.VMEM((rows, hidden), BF),
             jax.ShapeDtypeStruct((rows, hidden), BF),
         ),
-        in_specs=[VM] * 4,
+        in_specs=[VM] * 7,
         out_specs=(VM,) * 6,
+        input_output_aliases={4: 2, 5: 3, 6: 4},
         compiler_params=params(32),
         cost_estimate=cost(8 * rows * width * hidden, 4 * width * hidden),
         name="expert",
-    )(mine, theirs, w_in, w_out)
+    )(theirs, w_in, w_out, slope, slot, cot, act)
 
 
 def join_kernel(pieces, images, keep, got, send):
@@ -323,23 +347,32 @@
     )(back, tok, cot, disp, comb)
 
 
+def run_now(work):
+    pl.when(pl.program_id(0) >= 0)(work)
+
+
+def weight_rows(left, right, held, out, sems, first):
+    parts = sems.shape[0]
+    size = held.shape[0] // parts
+    copies = [
+        pltpu.make_async_copy(
+            held.at[pl.ds(i * size, size)], out.at[pl.ds(first + i * size, size)], sems.at[i]
+        )
+        for i in range(parts)
+    ]
+    for i in range(parts):
+        at = first + i * size
+        held[pl.ds(i * size, size), :] = mm(left[:, at : at + size], right[...], 0, 0).astype(BF)
+        run_now(copies[i].start)
+    return copies
+
+
 def weight_kernel(left, right, out, held, sems):
-    parts = sems.shape[0]
-    size = out.shape[0] // parts
-    for i in range(parts):
-        rows = pl.ds(i * size, size)
-        held[rows, :] = mm(left[:, i * size : (i + 1) * size], right[...], 0, 0).astype(BF)
-
-        @pl.when(pl.program_id(0) >= 0)
-        def _():
-            pltpu.make_async_copy(held.at[rows], out.at[rows], sems.at[i]).start()
-
-    for i in range(parts):
-        rows = pl.ds(i * size, size)
-        pltpu.make_async_copy(held.at[rows], out.at[rows], sems.at[i]).wait()
-
-
-def weight_grad(left, right):
+    for copy in weight_rows(left, right, held, out, sems, 0):
+        copy.wait()
+
+
+def weight_grad(left, right, count):
     shape = (left.shape[1], right.shape[1])
     return pl.pallas_call(
         weight_kernel,
@@ -347,31 +380,48 @@
         out_shape=jax.ShapeDtypeStruct(shape, BF),
         in_specs=[VM] * 2,
         out_specs=HBM,
-        scratch_shapes=[pltpu.VMEM(shape, BF), pltpu.SemaphoreType.DMA((8,))],
+        scratch_shapes=[pltpu.VMEM((count, shape[1]), BF), pltpu.SemaphoreType.DMA((count // 256,))],
         compiler_params=params(16),
-        cost_estimate=cost(2 * left.size * right.shape[1], 2 * shape[0] * shape[1]),
+        cost_estimate=cost(2 * left.shape[0] * count * shape[1], 2 * count * shape[1]),
     )(left, right)
 
 
-def tokens_kernel(disp, lgrad, sgrad, router, out):
+def tokens_kernel(
+    disp, lgrad, sgrad, router, left, right, begun, out, full, made, held, out_sems, sems
+):
+    del begun
+    copies = []
     for n in range(disp.shape[0]):
-        left = jnp.concatenate([disp[n].astype(BF), lgrad[n]], axis=0)
-        right = jnp.concatenate([sgrad[n], router[...]], axis=0)
-        out[n] = mm(left, right, 0, 0).astype(BF)
-
-
-def token_grads(disp, lgrad, sgrad, router_t):
+        both = jnp.concatenate([disp[n].astype(BF), lgrad[n]], axis=0)
+        made[n] = mm(both, jnp.concatenate([sgrad[n], router[...]], axis=0), 0, 0).astype(BF)
+        copies.append(pltpu.make_async_copy(made.at[n], out.at[n], out_sems.at[n]))
+        run_now(copies[n].start)
+    copies += weight_rows(left, right, held, full, sems, full.shape[0] - held.shape[0])
+    for copy in copies:
+        copy.wait()
+
+
+def token_grads(disp, lgrad, sgrad, router_t, left, right, begun, count):
     images, experts, toks = disp.shape
     width = router_t.shape[1]
+    shape = (images, toks, width)
     return pl.pallas_call(
         tokens_kernel,
-        out_shape=jax.ShapeDtypeStruct((images, toks, width), BF),
-        in_specs=[VM] * 4,
-        out_specs=VM,
+        grid=(1,),
+        out_shape=(jax.ShapeDtypeStruct(shape, BF), jax.ShapeDtypeStruct(begun.shape, BF)),
+        in_specs=[VM] * 6 + [HBM],
+        out_specs=(HBM, HBM),
+        scratch_shapes=[
+            pltpu.VMEM(shape, BF),
+            pltpu.VMEM((count, begun.shape[1]), BF),
+            pltpu.SemaphoreType.DMA((images,)),
+            pltpu.SemaphoreType.DMA((count // 256,)),
+        ],
+        input_output_aliases={6: 1},
         compiler_params=params(16),
         cost_estimate=cost(4 * images * toks * width * experts, 2 * images * toks * width),
         name="token_grads",
-    )(disp, lgrad, sgrad, router_t)
+    )(disp, lgrad, sgrad, router_t, left, right, in_hbm(begun))
 
 
 def rounded(x):
@@ -417,17 +467,20 @@
         )
         mine = exchange(send)
         theirs = swap_pair(mine)
-        held_out = fetch(w_out[0])
+        held_out, slot_rows, cot_rows, act, slope = run_own(mine, held_in, w_out[0], images)
         keep, give, slot_rows, cot_rows, act, hgrad = run_expert(
-            mine, theirs, held_in, held_out, images
+            theirs, held_in, held_out, slope, slot_rows, cot_rows, act, images
         )
         got = swap_pair(give)
         joined = join(keep, got, images)
         back = exchange(joined)
-        grad_in = weight_grad(slot_rows, hgrad)
-        grad_out = weight_grad(act, cot_rows)
+        grad_in = weight_grad(slot_rows, hgrad, slot_rows.shape[1])
+        half = act.shape[1] // 2
+        begun = weight_grad(act, cot_rows, half)
         part, lgrad, sgrad = logit_grads(back, tok, cot, disp, comb)
-        tokens_grad = token_grads(disp, lgrad, sgrad, router_t)
+        tokens_grad, grad_out = token_grads(
+            disp, lgrad, sgrad, router_t, act, cot_rows, begun, half
+        )
         router_grad = all_sum(part, sizes["expert"]).T
         return tokens_grad, grad_in[None], grad_out[None], router_grad
 

time: 70.4 us -> 69.8 us (level)
  no operation moved by 1% of the time
where the time goes in v3:
time: 69.8 us; the launch traced here: 69.6 us
  blocking collectives  37.3 us (53%)
  Pallas kernels  19.6 us (28%)
  starting transfers between devices  8.64 us (12%)
  waiting for transfers between devices  2.56 us (4%)
  between operations  0.77 us (1%)
  other arithmetic  0.72 us (1%)
    all_to_all x2, blocking collectives, exchange(): lax.all_to_all(blocks, 'expert', split_axis=0, concat_axis=0, tiled=True)  37.3 us
    ppermute x6, starting transfers between devices, toward(): lax.ppermute(x, 'expert', [(i, i ^ mask) for i in range(size)]).astype(F32)  8.01 us
    pallas_call x1, Pallas kernels, run_expert(): pl.pallas_call(functools.partial(expert_kernel, pieces, images), out_shap...  4.3 us
    pallas_call x2, Pallas kernels, weight_grad(): pl.pallas_call(weight_kernel, grid=(1,), out_shape=jax.ShapeDtypeStruct(s...  4.17 us
    pallas_call x1, Pallas kernels, make_slots(): pl.pallas_call(functools.partial(slots_kernel, pieces, 3), out_shape=(plt...  4.01 us
    ppermute x3, waiting for transfers between devices, swap_pair(): return lax.ppermute(x, 'pair', [(0, 1), (1, 0)])  2.55 us
    pallas_call x1, Pallas kernels, token_grads(): pl.pallas_call(tokens_kernel, grid=(1,), out_shape=(jax.ShapeDtypeStruct(...  2.53 us
    pallas_call x1, Pallas kernels, run_own(): pl.pallas_call(functools.partial(own_kernel, pieces, images), out_shape=(...  2.21 us
  transfers between devices with their start and end apart: 9, of which 2 were waited for; matrix products, arithmetic and copies ran while one was open for 0% of the time, Pallas kernels for 13%

profile of v3, /device:TPU:0, one launch (start us, length us, event | category | flops | bytes accessed | tf_op | source)
XLA Modules:
  0.0 69.6 jit_solution(12796481841350868560)
XLA Ops:
  0.6 4.0 %slots.1 = (bf16[384,512]{1,0:T(8,128)(2,1)S(1)}, f32[6,16,196]{2,1,0:T(8,128)S(1)}, f32[6,16,196]{2,1,0:T(8,128)S(1)}, bf16[16,1024]{1,0:T(8,128)(2,1)S(1)}, bf...) custom-call(bf16[6,196,1024]{2,1,0:T(8,128)(2,1)} %tok_hbm.1, ...), custom_call_target="tpu_custom_call" | custom-call | flops 115605504 | bytes 4816896 | tf_op jit(solution)/shard_map/slots/pallas_call | solution.py:125
  4.7 20.8 %all_to_all.10 = bf16[16,24,512]{2,1,0:T(8,128)(2,1)S(1)} all-to-all(bf16[16,24,512]{2,1,0:T(8,128)(2,1)S(1)} %bitcast.15), channel_id=1, replica_groups=mesh['expert'=16,'pair'=2] {'expert'}, dimensions={0} | all-to-all | bytes 786432 | tf_op jit(solution)/shard_map/all_to_all | solution.py:461
  25.4 0.0 collective-permute-start
  25.4 2.2 %own.1 = (bf16[2048,1024]{1,0:T(8,128)(2,1)S(1)}, bf16[192,1024]{1,0:T(8,128)(2,1)S(1)}, bf16[192,1024]{1,0:T(8,128)(2,1)S(1)}, bf16[192,2048]{1,0:T(8,128)(2,1)S(1)}, f32[96,2048]{1,0:T(8,128)S(1)}) custom-call(bf16[384,512]{1,0:T(8,128)(2,1)S(1)} %bitcast.12, bf16[1024,2048]{1,0:T(8,128)(2,1)S(1)} %get-tuple-element.29.w_in, bf16[2048,1024]{1,0:T(8,128)(2,1)} %bitcast.18), custom_call_target="tpu_custom_call" | custom-call | flops 402653184 | bytes 4194304 | tf_op jit(solution)/shard_map/own/pallas_call | solution.py:198
  27.6 0.0 collective-permute-done.theirs
  27.7 4.3 %expert.1 = (f32[192,1024]{1,0:T(8,128)S(1)}, bf16[192,1024]{1,0:T(8,128)(2,1)S(1)}, bf16[192,1024]{1,0:T(8,128)(2,1)S(1)}, bf16[192,1024]{1,0:T(8,128)(2,1)S(1)...) custom-call(bf16[384,512]{1,0:T(8,128)(2,1)S(1)} %collective-permute, ...), custom_call_target="tpu_custom_call", output_to_operand_aliasing={{2}: (4, {}), {3}: (5, {}), {4}: (6, {})} | custom-call | flops 3221225472 | bytes 8388608 | tf_op jit(solution)/shard_map/expert/pallas_call | solution.py:244
  32.0 0.6 collective-permute-start.1
  32.5 1.3 %collective-permute-done.1.got = bf16[192,1024]{1,0:T(8,128)(2,1)S(1)} collective-permute-done((bf16[192,1024]{1,0:T(8,128)(2,1)S(1)}, bf16[192,1024]{1,0:T(8,128)(2,1)S(1)}, u32[]{:S(2)}, u32[]{:S(2)}) %collective-permute-start.1) | collective-permute-done | bytes 393248 | tf_op jit(solution)/shard_map/ppermute | solution.py:432
  33.9 0.4 join.1
  34.3 16.5 %all_to_all.11 = bf16[16,24,512]{2,1,0:T(8,128)(2,1)S(1)} all-to-all(bf16[16,24,512]{2,1,0:T(8,128)(2,1)S(1)} %bitcast.13), channel_id=1, replica_groups=mesh['expert'=16,'pair'=2] {'expert'}, dimensions={0} | all-to-all | bytes 786432 | tf_op jit(solution)/shard_map/all_to_all | solution.py:461
  50.8 2.0 %logit_grads.1 = (f32[16,1024]{1,0:T(8,128)S(1)}, bf16[6,16,196]{2,1,0:T(8,128)(2,1)S(1)}, bf16[6,16,1024]{2,1,0:T(8,128)(2,1)S(1)}) custom-call(bf16[384,512]{1,0:T(8,128)(2,1)S(1)} %bitcast.14, bf16[6,196,1024]{2,1,0:T(8,128)(2,1)S(1)} %get-tuple-element.37.tok, bf16[6,196,1024]{2,1,0:T(8,128)(2,1)S(1)} %get-tuple-element.38.cot, ...), custom_call_target="tpu_custom_call" | custom-call | flops 115605504 | bytes 4816896 | tf_op jit(solution)/shard_map/logit_grads/pallas_call | solution.py:334
  52.8 0.1 collective-permute-start.2
  52.9 1.2 %collective-permute-done.2 = bf16[16,1024]{1,0:T(8,128)(2,1)S(1)} collective-permute-done((bf16[16,1024]{1,0:T(8,128)(2,1)S(1)}, bf16[16,1024]{1,0:T(8,128)(2,1)S(1)}, u32[]{:S(2)}, u32[]{:S(2)}) %collective-permute-start.2) | collective-permute-done | bytes 32800 | tf_op jit(solution)/shard_map/ppermute | solution.py:432
  54.1 0.9 %collective-permute-start.5 = (bf16[16,1024]{1,0:T(8,128)(2,1)S(1)}, bf16[16,1024]{1,0:T(8,128)(2,1)S(1)}, u32[]{:S(2)}, u32[]{:S(2)}) collective-permute-start(bf16[16,1024]{1,0:T(8,128)(2,1)S(1)} %fusion), channel_id=1, source_target_pairs={{0,6},{2,4},{4,2},{6,0},{8,14},{10,12},{12,10},{14,8},{16,22},{18,... | collective-permute-start | bytes 98312 | tf_op jit(solution)/shard_map/ppermute | solution.py:436
  55.0 1.2 %collective-permute-start.4 = (bf16[16,1024]{1,0:T(8,128)(2,1)S(1)}, bf16[16,1024]{1,0:T(8,128)(2,1)S(1)}, u32[]{:S(2)}, u32[]{:S(2)}) collective-permute-start(bf16[16,1024]{1,0:T(8,128)(2,1)S(1)} %fusion), channel_id=1, source_target_pairs={{0,4},{2,6},{4,0},{6,2},{8,12},{10,14},{12,8},{14,10},{16,20},{18,... | collective-permute-start | bytes 98312 | tf_op jit(solution)/shard_map/ppermute | solution.py:436
  56.1 1.5 %collective-permute-start.3 = (bf16[16,1024]{1,0:T(8,128)(2,1)S(1)}, bf16[16,1024]{1,0:T(8,128)(2,1)S(1)}, u32[]{:S(2)}, u32[]{:S(2)}) collective-permute-start(bf16[16,1024]{1,0:T(8,128)(2,1)S(1)} %fusion), channel_id=1, source_target_pairs={{0,2},{2,0},{4,6},{6,4},{8,10},{10,8},{12,14},{14,12},{16,18},{18,... | collective-permute-start | bytes 98312 | tf_op jit(solution)/shard_map/ppermute | solution.py:436
  57.6 2.5 %shard_map.85 = bf16[1024,2048]{1,0:T(8,128)(2,1)} custom-call(bf16[192,1024]{1,0:T(8,128)(2,1)S(1)} %get-tuple-element.46.left, bf16[192,2048]{1,0:T(8,128)(2,1)S(1)} %get-tuple-element.47.right), custom_call_target="tpu_custom_call" | custom-call | flops 805306368 | bytes 4194304 | tf_op jit(solution)/shard_map/pallas_call | solution.py:377
  60.1 0.0 collective-permute-done.5
  60.1 0.0 collective-permute-done.4
  60.1 0.0 collective-permute-done.3
  60.2 1.6 %collective-permute-start.8 = (bf16[16,1024]{1,0:T(8,128)(2,1)S(1)}, bf16[16,1024]{1,0:T(8,128)(2,1)S(1)}, u32[]{:S(2)}, u32[]{:S(2)}) collective-permute-start(bf16[16,1024]{1,0:T(8,128)(2,1)S(1)} %fusion.1), channel_id=1, source_target_pairs={{0,24},{2,26},{4,28},{6,30},{8,16},{10,18},{12,20},{14,22},{16,8},... | collective-permute-start | bytes 98312 | tf_op jit(solution)/shard_map/ppermute | solution.py:436
  61.8 1.0 %collective-permute-start.7 = (bf16[16,1024]{1,0:T(8,128)(2,1)S(1)}, bf16[16,1024]{1,0:T(8,128)(2,1)S(1)}, u32[]{:S(2)}, u32[]{:S(2)}) collective-permute-start(bf16[16,1024]{1,0:T(8,128)(2,1)S(1)} %fusion.1), channel_id=1, source_target_pairs={{0,16},{2,18},{4,20},{6,22},{8,24},{10,26},{12,28},{14,30},{16,0},... | collective-permute-start | bytes 98312 | tf_op jit(solution)/shard_map/ppermute | solution.py:436
  62.8 1.8 %collective-permute-start.6 = (bf16[16,1024]{1,0:T(8,128)(2,1)S(1)}, bf16[16,1024]{1,0:T(8,128)(2,1)S(1)}, u32[]{:S(2)}, u32[]{:S(2)}) collective-permute-start(bf16[16,1024]{1,0:T(8,128)(2,1)S(1)} %fusion.1), channel_id=1, source_target_pairs={{0,8},{2,10},{4,12},{6,14},{8,0},{10,2},{12,4},{14,6},{16,24},{18,... | collective-permute-start | bytes 98312 | tf_op jit(solution)/shard_map/ppermute | solution.py:436
  64.7 1.7 %shard_map.84.begun = bf16[2048,1024]{1,0:T(8,128)(2,1)} custom-call(bf16[192,2048]{1,0:T(8,128)(2,1)S(1)} %get-tuple-element.43.left, bf16[192,1024]{1,0:T(8,128)(2,1)S(1)} %get-tuple-element.44.right), custom_call_target="tpu_custom_call" | custom-call | flops 402653184 | bytes 2097152 | tf_op jit(solution)/shard_map/pallas_call | solution.py:377
  66.3 2.5 %token_grads.1 = (bf16[6,196,1024]{2,1,0:T(8,128)(2,1)}, bf16[2048,1024]{1,0:T(8,128)(2,1)}) custom-call(f32[6,16,196]{2,1,0:T(8,128)S(1)} %get-tuple-element.27.disp, bf16[6,16,196]{2,1,0:T(8,128)(2,1)S(1)} %get-tuple-element.40.lgrad, bf16[6,16,1024]{2,1,0:T(8,128)(2,1)S(1)} %get-tuple-element.41.sgrad, ...), custom_call_target="tpu_custom_call", output_to_operand_aliasing={{1}: (6, {})} | custom-call | flops 77070336 | bytes 2408448 | tf_op jit(solution)/shard_map/token_grads/pallas_call | solution.py:408
  68.9 0.0 collective-permute-done.8
  68.9 0.0 collective-permute-done.7
  68.9 0.0 collective-permute-done.6
  68.9 0.7 add_bitcast_fusion
  (3 shorter events, 0.0 us)
Async XLA Ops:
  25.4 2.2 %collective-permute-start = (bf16[384,512]{1,0:T(8,128)(2,1)S(1)}, bf16[384,512]{1,0:T(8,128)(2,1)S(1)}, u32[]{:S(2)}, u32[]{:S(2)}) collective-permute-start(bf16[384,512]{1,0:T(8,128)(2,1)S(1)} %bitcast.11), channel_id=1, source_target_pairs={{0,1},{1,0},{2,3},{3,2},{4,5},{5,4},{6,7},{7,6},{8,9},{9,8},{10,11... | collective-permute-start | bytes 1179656 | tf_op jit(solution)/shard_map/ppermute | solution.py:432
  32.0 1.9 %collective-permute-start.1 = (bf16[192,1024]{1,0:T(8,128)(2,1)S(1)}, bf16[192,1024]{1,0:T(8,128)(2,1)S(1)}, u32[]{:S(2)}, u32[]{:S(2)}) collective-permute-start(bf16[192,1024]{1,0:T(8,128)(2,1)S(1)} %get-tuple-element.36), channel_id=1, source_target_pairs={{0,1},{1,0},{2,3},{3,2},{4,5},{5,4},{6,7},{7,6},{8,9},{9,8},{10,11... | collective-permute-start | bytes 1179656 | tf_op jit(solution)/shard_map/ppermute | solution.py:432
  52.8 1.3 %collective-permute-start.2 = (bf16[16,1024]{1,0:T(8,128)(2,1)S(1)}, bf16[16,1024]{1,0:T(8,128)(2,1)S(1)}, u32[]{:S(2)}, u32[]{:S(2)}) collective-permute-start(bf16[16,1024]{1,0:T(8,128)(2,1)S(1)} %reduce-precision_convert_fusion), channel_id=1, source_target_pairs={{0,1},{1,0},{2,3},{3,2},{4,5},{5,4},{6,7},{7,6},{8,9},{9,8},{10,11... | collective-permute-start | bytes 98312 | tf_op jit(solution)/shard_map/ppermute | solution.py:432
  54.1 6.1 %collective-permute-start.5 = (bf16[16,1024]{1,0:T(8,128)(2,1)S(1)}, bf16[16,1024]{1,0:T(8,128)(2,1)S(1)}, u32[]{:S(2)}, u32[]{:S(2)}) collective-permute-start(bf16[16,1024]{1,0:T(8,128)(2,1)S(1)} %fusion), channel_id=1, source_target_pairs={{0,6},{2,4},{4,2},{6,0},{8,14},{10,12},{12,10},{14,8},{16,22},{18,... | collective-permute-start | bytes 98312 | tf_op jit(solution)/shard_map/ppermute | solution.py:436
  55.0 5.2 %collective-permute-start.4 = (bf16[16,1024]{1,0:T(8,128)(2,1)S(1)}, bf16[16,1024]{1,0:T(8,128)(2,1)S(1)}, u32[]{:S(2)}, u32[]{:S(2)}) collective-permute-start(bf16[16,1024]{1,0:T(8,128)(2,1)S(1)} %fusion), channel_id=1, source_target_pairs={{0,4},{2,6},{4,0},{6,2},{8,12},{10,14},{12,8},{14,10},{16,20},{18,... | collective-permute-start | bytes 98312 | tf_op jit(solution)/shard_map/ppermute | solution.py:436
  56.1 4.0 %collective-permute-start.3 = (bf16[16,1024]{1,0:T(8,128)(2,1)S(1)}, bf16[16,1024]{1,0:T(8,128)(2,1)S(1)}, u32[]{:S(2)}, u32[]{:S(2)}) collective-permute-start(bf16[16,1024]{1,0:T(8,128)(2,1)S(1)} %fusion), channel_id=1, source_target_pairs={{0,2},{2,0},{4,6},{6,4},{8,10},{10,8},{12,14},{14,12},{16,18},{18,... | collective-permute-start | bytes 98312 | tf_op jit(solution)/shard_map/ppermute | solution.py:436
  60.2 8.7 %collective-permute-start.8 = (bf16[16,1024]{1,0:T(8,128)(2,1)S(1)}, bf16[16,1024]{1,0:T(8,128)(2,1)S(1)}, u32[]{:S(2)}, u32[]{:S(2)}) collective-permute-start(bf16[16,1024]{1,0:T(8,128)(2,1)S(1)} %fusion.1), channel_id=1, source_target_pairs={{0,24},{2,26},{4,28},{6,30},{8,16},{10,18},{12,20},{14,22},{16,8},... | collective-permute-start | bytes 98312 | tf_op jit(solution)/shard_map/ppermute | solution.py:436
  61.8 7.1 %collective-permute-start.7 = (bf16[16,1024]{1,0:T(8,128)(2,1)S(1)}, bf16[16,1024]{1,0:T(8,128)(2,1)S(1)}, u32[]{:S(2)}, u32[]{:S(2)}) collective-permute-start(bf16[16,1024]{1,0:T(8,128)(2,1)S(1)} %fusion.1), channel_id=1, source_target_pairs={{0,16},{2,18},{4,20},{6,22},{8,24},{10,26},{12,28},{14,30},{16,0},... | collective-permute-start | bytes 98312 | tf_op jit(solution)/shard_map/ppermute | solution.py:436
  62.8 6.1 %collective-permute-start.6 = (bf16[16,1024]{1,0:T(8,128)(2,1)S(1)}, bf16[16,1024]{1,0:T(8,128)(2,1)S(1)}, u32[]{:S(2)}, u32[]{:S(2)}) collective-permute-start(bf16[16,1024]{1,0:T(8,128)(2,1)S(1)} %fusion.1), channel_id=1, source_target_pairs={{0,8},{2,10},{4,12},{6,14},{8,0},{10,2},{12,4},{14,6},{16,24},{18,... | collective-permute-start | bytes 98312 | tf_op jit(solution)/shard_map/ppermute | solution.py:436

commit v4 on v3

--- a/solution.py
+++ b/solution.py
@@ -138,9 +138,9 @@
         scratch_shapes=[
             pltpu.VMEM((2 * images * experts, width), BF),
             pltpu.SemaphoreType.DMA((images,)),
-            pltpu.SemaphoreType.DMA((images,)),
+            pltpu.SemaphoreType.DMA((math.gcd(images, 2),)),
             pltpu.SemaphoreType.DMA,
-            pltpu.SemaphoreType.DMA((8,)),
+            pltpu.SemaphoreType.DMA((2,)),
         ],
         compiler_params=params(16),
         cost_estimate=cost(6 * images * toks * width * experts, 4 * images * toks * width),
@@ -206,7 +206,7 @@
         ),
         in_specs=[VM, VM, HBM],
         out_specs=(VM,) * 5,
-        scratch_shapes=[pltpu.SemaphoreType.DMA((8,))],
+        scratch_shapes=[pltpu.SemaphoreType.DMA((2,))],
         compiler_params=params(16),
         cost_estimate=cost(rows * width * hidden, 2 * w_out.size),
         name="own",

time: 69.8 us -> 69.7 us (level)
  no operation moved by 1% of the time
where the time goes in v4:
time: 69.7 us; the launch traced here: 69.5 us
  blocking collectives  37.3 us (54%)
  Pallas kernels  19.5 us (28%)
  starting transfers between devices  8.66 us (12%)
  waiting for transfers between devices  2.56 us (4%)
  between operations  0.77 us (1%)
  other arithmetic  0.72 us (1%)
    all_to_all x2, blocking collectives, exchange(): lax.all_to_all(blocks, 'expert', split_axis=0, concat_axis=0, tiled=True)  37.3 us
    ppermute x6, starting transfers between devices, toward(): lax.ppermute(x, 'expert', [(i, i ^ mask) for i in range(size)]).astype(F32)  8.01 us
    pallas_call x1, Pallas kernels, run_expert(): pl.pallas_call(functools.partial(expert_kernel, pieces, images), out_shap...  4.28 us
    pallas_call x2, Pallas kernels, weight_grad(): pl.pallas_call(weight_kernel, grid=(1,), out_shape=jax.ShapeDtypeStruct(s...  4.17 us
    pallas_call x1, Pallas kernels, make_slots(): pl.pallas_call(functools.partial(slots_kernel, pieces, 3), out_shape=(plt...  3.91 us
    ppermute x3, waiting for transfers between devices, swap_pair(): return lax.ppermute(x, 'pair', [(0, 1), (1, 0)])  2.55 us
    pallas_call x1, Pallas kernels, token_grads(): pl.pallas_call(tokens_kernel, grid=(1,), out_shape=(jax.ShapeDtypeStruct(...  2.53 us
    pallas_call x1, Pallas kernels, run_own(): pl.pallas_call(functools.partial(own_kernel, pieces, images), out_shape=(...  2.24 us
  transfers between devices with their start and end apart: 9, of which 2 were waited for; matrix products, arithmetic and copies ran while one was open for 0% of the time, Pallas kernels for 13%

profile of v4, /device:TPU:0, one launch (start us, length us, event | category | flops | bytes accessed | tf_op | source)
XLA Modules:
  0.0 69.5 jit_solution(12290139040574934880)
XLA Ops:
  0.6 3.9 %slots.1 = (bf16[384,512]{1,0:T(8,128)(2,1)S(1)}, f32[6,16,196]{2,1,0:T(8,128)S(1)}, f32[6,16,196]{2,1,0:T(8,128)S(1)}, bf16[16,1024]{1,0:T(8,128)(2,1)S(1)}, bf...) custom-call(bf16[6,196,1024]{2,1,0:T(8,128)(2,1)} %tok_hbm.1, ...), custom_call_target="tpu_custom_call" | custom-call | flops 115605504 | bytes 4816896 | tf_op jit(solution)/shard_map/slots/pallas_call | solution.py:125
  4.6 20.8 %all_to_all.10 = bf16[16,24,512]{2,1,0:T(8,128)(2,1)S(1)} all-to-all(bf16[16,24,512]{2,1,0:T(8,128)(2,1)S(1)} %bitcast.15), channel_id=1, replica_groups=mesh['expert'=16,'pair'=2] {'expert'}, dimensions={0} | all-to-all | bytes 786432 | tf_op jit(solution)/shard_map/all_to_all | solution.py:461
  25.3 0.0 collective-permute-start
  25.3 2.2 %own.1 = (bf16[2048,1024]{1,0:T(8,128)(2,1)S(1)}, bf16[192,1024]{1,0:T(8,128)(2,1)S(1)}, bf16[192,1024]{1,0:T(8,128)(2,1)S(1)}, bf16[192,2048]{1,0:T(8,128)(2,1)S(1)}, f32[96,2048]{1,0:T(8,128)S(1)}) custom-call(bf16[384,512]{1,0:T(8,128)(2,1)S(1)} %bitcast.12, bf16[1024,2048]{1,0:T(8,128)(2,1)S(1)} %get-tuple-element.29.w_in, bf16[2048,1024]{1,0:T(8,128)(2,1)} %bitcast.18), custom_call_target="tpu_custom_call" | custom-call | flops 402653184 | bytes 4194304 | tf_op jit(solution)/shard_map/own/pallas_call | solution.py:198
  27.6 0.0 collective-permute-done.theirs
  27.6 4.3 %expert.1 = (f32[192,1024]{1,0:T(8,128)S(1)}, bf16[192,1024]{1,0:T(8,128)(2,1)S(1)}, bf16[192,1024]{1,0:T(8,128)(2,1)S(1)}, bf16[192,1024]{1,0:T(8,128)(2,1)S(1)...) custom-call(bf16[384,512]{1,0:T(8,128)(2,1)S(1)} %collective-permute, ...), custom_call_target="tpu_custom_call", output_to_operand_aliasing={{2}: (4, {}), {3}: (5, {}), {4}: (6, {})} | custom-call | flops 3221225472 | bytes 8388608 | tf_op jit(solution)/shard_map/expert/pallas_call | solution.py:244
  31.9 0.6 collective-permute-start.1
  32.5 1.3 %collective-permute-done.1.got = bf16[192,1024]{1,0:T(8,128)(2,1)S(1)} collective-permute-done((bf16[192,1024]{1,0:T(8,128)(2,1)S(1)}, bf16[192,1024]{1,0:T(8,128)(2,1)S(1)}, u32[]{:S(2)}, u32[]{:S(2)}) %collective-permute-start.1) | collective-permute-done | bytes 393248 | tf_op jit(solution)/shard_map/ppermute | solution.py:432
  33.8 0.4 join.1
  34.2 16.5 %all_to_all.11 = bf16[16,24,512]{2,1,0:T(8,128)(2,1)S(1)} all-to-all(bf16[16,24,512]{2,1,0:T(8,128)(2,1)S(1)} %bitcast.13), channel_id=1, replica_groups=mesh['expert'=16,'pair'=2] {'expert'}, dimensions={0} | all-to-all | bytes 786432 | tf_op jit(solution)/shard_map/all_to_all | solution.py:461
  50.7 2.0 %logit_grads.1 = (f32[16,1024]{1,0:T(8,128)S(1)}, bf16[6,16,196]{2,1,0:T(8,128)(2,1)S(1)}, bf16[6,16,1024]{2,1,0:T(8,128)(2,1)S(1)}) custom-call(bf16[384,512]{1,0:T(8,128)(2,1)S(1)} %bitcast.14, bf16[6,196,1024]{2,1,0:T(8,128)(2,1)S(1)} %get-tuple-element.37.tok, bf16[6,196,1024]{2,1,0:T(8,128)(2,1)S(1)} %get-tuple-element.38.cot, ...), custom_call_target="tpu_custom_call" | custom-call | flops 115605504 | bytes 4816896 | tf_op jit(solution)/shard_map/logit_grads/pallas_call | solution.py:334
  52.7 0.1 collective-permute-start.2
  52.8 1.2 %collective-permute-done.2 = bf16[16,1024]{1,0:T(8,128)(2,1)S(1)} collective-permute-done((bf16[16,1024]{1,0:T(8,128)(2,1)S(1)}, bf16[16,1024]{1,0:T(8,128)(2,1)S(1)}, u32[]{:S(2)}, u32[]{:S(2)}) %collective-permute-start.2) | collective-permute-done | bytes 32800 | tf_op jit(solution)/shard_map/ppermute | solution.py:432
  54.0 0.9 %collective-permute-start.5 = (bf16[16,1024]{1,0:T(8,128)(2,1)S(1)}, bf16[16,1024]{1,0:T(8,128)(2,1)S(1)}, u32[]{:S(2)}, u32[]{:S(2)}) collective-permute-start(bf16[16,1024]{1,0:T(8,128)(2,1)S(1)} %fusion), channel_id=1, source_target_pairs={{0,6},{2,4},{4,2},{6,0},{8,14},{10,12},{12,10},{14,8},{16,22},{18,... | collective-permute-start | bytes 98312 | tf_op jit(solution)/shard_map/ppermute | solution.py:436
  54.9 1.2 %collective-permute-start.4 = (bf16[16,1024]{1,0:T(8,128)(2,1)S(1)}, bf16[16,1024]{1,0:T(8,128)(2,1)S(1)}, u32[]{:S(2)}, u32[]{:S(2)}) collective-permute-start(bf16[16,1024]{1,0:T(8,128)(2,1)S(1)} %fusion), channel_id=1, source_target_pairs={{0,4},{2,6},{4,0},{6,2},{8,12},{10,14},{12,8},{14,10},{16,20},{18,... | collective-permute-start | bytes 98312 | tf_op jit(solution)/shard_map/ppermute | solution.py:436
  56.1 1.5 %collective-permute-start.3 = (bf16[16,1024]{1,0:T(8,128)(2,1)S(1)}, bf16[16,1024]{1,0:T(8,128)(2,1)S(1)}, u32[]{:S(2)}, u32[]{:S(2)}) collective-permute-start(bf16[16,1024]{1,0:T(8,128)(2,1)S(1)} %fusion), channel_id=1, source_target_pairs={{0,2},{2,0},{4,6},{6,4},{8,10},{10,8},{12,14},{14,12},{16,18},{18,... | collective-permute-start | bytes 98312 | tf_op jit(solution)/shard_map/ppermute | solution.py:436
  57.5 2.5 %shard_map.85 = bf16[1024,2048]{1,0:T(8,128)(2,1)} custom-call(bf16[192,1024]{1,0:T(8,128)(2,1)S(1)} %get-tuple-element.46.left, bf16[192,2048]{1,0:T(8,128)(2,1)S(1)} %get-tuple-element.47.right), custom_call_target="tpu_custom_call" | custom-call | flops 805306368 | bytes 4194304 | tf_op jit(solution)/shard_map/pallas_call | solution.py:377
  60.0 0.0 collective-permute-done.5
  60.1 0.0 collective-permute-done.4
  60.1 0.0 collective-permute-done.3
  60.1 1.6 %collective-permute-start.8 = (bf16[16,1024]{1,0:T(8,128)(2,1)S(1)}, bf16[16,1024]{1,0:T(8,128)(2,1)S(1)}, u32[]{:S(2)}, u32[]{:S(2)}) collective-permute-start(bf16[16,1024]{1,0:T(8,128)(2,1)S(1)} %fusion.1), channel_id=1, source_target_pairs={{0,24},{2,26},{4,28},{6,30},{8,16},{10,18},{12,20},{14,22},{16,8},... | collective-permute-start | bytes 98312 | tf_op jit(solution)/shard_map/ppermute | solution.py:436
  61.7 1.0 %collective-permute-start.7 = (bf16[16,1024]{1,0:T(8,128)(2,1)S(1)}, bf16[16,1024]{1,0:T(8,128)(2,1)S(1)}, u32[]{:S(2)}, u32[]{:S(2)}) collective-permute-start(bf16[16,1024]{1,0:T(8,128)(2,1)S(1)} %fusion.1), channel_id=1, source_target_pairs={{0,16},{2,18},{4,20},{6,22},{8,24},{10,26},{12,28},{14,30},{16,0},... | collective-permute-start | bytes 98312 | tf_op jit(solution)/shard_map/ppermute | solution.py:436
  62.7 1.8 %collective-permute-start.6 = (bf16[16,1024]{1,0:T(8,128)(2,1)S(1)}, bf16[16,1024]{1,0:T(8,128)(2,1)S(1)}, u32[]{:S(2)}, u32[]{:S(2)}) collective-permute-start(bf16[16,1024]{1,0:T(8,128)(2,1)S(1)} %fusion.1), channel_id=1, source_target_pairs={{0,8},{2,10},{4,12},{6,14},{8,0},{10,2},{12,4},{14,6},{16,24},{18,... | collective-permute-start | bytes 98312 | tf_op jit(solution)/shard_map/ppermute | solution.py:436
  64.6 1.7 %shard_map.84.begun = bf16[2048,1024]{1,0:T(8,128)(2,1)} custom-call(bf16[192,2048]{1,0:T(8,128)(2,1)S(1)} %get-tuple-element.43.left, bf16[192,1024]{1,0:T(8,128)(2,1)S(1)} %get-tuple-element.44.right), custom_call_target="tpu_custom_call" | custom-call | flops 402653184 | bytes 2097152 | tf_op jit(solution)/shard_map/pallas_call | solution.py:377
  66.2 2.5 %token_grads.1 = (bf16[6,196,1024]{2,1,0:T(8,128)(2,1)}, bf16[2048,1024]{1,0:T(8,128)(2,1)}) custom-call(f32[6,16,196]{2,1,0:T(8,128)S(1)} %get-tuple-element.27.disp, bf16[6,16,196]{2,1,0:T(8,128)(2,1)S(1)} %get-tuple-element.40.lgrad, bf16[6,16,1024]{2,1,0:T(8,128)(2,1)S(1)} %get-tuple-element.41.sgrad, ...), custom_call_target="tpu_custom_call", output_to_operand_aliasing={{1}: (6, {})} | custom-call | flops 77070336 | bytes 2408448 | tf_op jit(solution)/shard_map/token_grads/pallas_call | solution.py:408
  68.8 0.0 collective-permute-done.8
  68.8 0.0 collective-permute-done.7
  68.8 0.0 collective-permute-done.6
  68.8 0.7 add_bitcast_fusion
  (3 shorter events, 0.0 us)
Async XLA Ops:
  25.3 2.3 %collective-permute-start = (bf16[384,512]{1,0:T(8,128)(2,1)S(1)}, bf16[384,512]{1,0:T(8,128)(2,1)S(1)}, u32[]{:S(2)}, u32[]{:S(2)}) collective-permute-start(bf16[384,512]{1,0:T(8,128)(2,1)S(1)} %bitcast.11), channel_id=1, source_target_pairs={{0,1},{1,0},{2,3},{3,2},{4,5},{5,4},{6,7},{7,6},{8,9},{9,8},{10,11... | collective-permute-start | bytes 1179656 | tf_op jit(solution)/shard_map/ppermute | solution.py:432
  31.9 1.9 %collective-permute-start.1 = (bf16[192,1024]{1,0:T(8,128)(2,1)S(1)}, bf16[192,1024]{1,0:T(8,128)(2,1)S(1)}, u32[]{:S(2)}, u32[]{:S(2)}) collective-permute-start(bf16[192,1024]{1,0:T(8,128)(2,1)S(1)} %get-tuple-element.36), channel_id=1, source_target_pairs={{0,1},{1,0},{2,3},{3,2},{4,5},{5,4},{6,7},{7,6},{8,9},{9,8},{10,11... | collective-permute-start | bytes 1179656 | tf_op jit(solution)/shard_map/ppermute | solution.py:432
  52.7 1.3 %collective-permute-start.2 = (bf16[16,1024]{1,0:T(8,128)(2,1)S(1)}, bf16[16,1024]{1,0:T(8,128)(2,1)S(1)}, u32[]{:S(2)}, u32[]{:S(2)}) collective-permute-start(bf16[16,1024]{1,0:T(8,128)(2,1)S(1)} %reduce-precision_convert_fusion), channel_id=1, source_target_pairs={{0,1},{1,0},{2,3},{3,2},{4,5},{5,4},{6,7},{7,6},{8,9},{9,8},{10,11... | collective-permute-start | bytes 98312 | tf_op jit(solution)/shard_map/ppermute | solution.py:432
  54.0 6.1 %collective-permute-start.5 = (bf16[16,1024]{1,0:T(8,128)(2,1)S(1)}, bf16[16,1024]{1,0:T(8,128)(2,1)S(1)}, u32[]{:S(2)}, u32[]{:S(2)}) collective-permute-start(bf16[16,1024]{1,0:T(8,128)(2,1)S(1)} %fusion), channel_id=1, source_target_pairs={{0,6},{2,4},{4,2},{6,0},{8,14},{10,12},{12,10},{14,8},{16,22},{18,... | collective-permute-start | bytes 98312 | tf_op jit(solution)/shard_map/ppermute | solution.py:436
  54.9 5.2 %collective-permute-start.4 = (bf16[16,1024]{1,0:T(8,128)(2,1)S(1)}, bf16[16,1024]{1,0:T(8,128)(2,1)S(1)}, u32[]{:S(2)}, u32[]{:S(2)}) collective-permute-start(bf16[16,1024]{1,0:T(8,128)(2,1)S(1)} %fusion), channel_id=1, source_target_pairs={{0,4},{2,6},{4,0},{6,2},{8,12},{10,14},{12,8},{14,10},{16,20},{18,... | collective-permute-start | bytes 98312 | tf_op jit(solution)/shard_map/ppermute | solution.py:436
  56.1 4.0 %collective-permute-start.3 = (bf16[16,1024]{1,0:T(8,128)(2,1)S(1)}, bf16[16,1024]{1,0:T(8,128)(2,1)S(1)}, u32[]{:S(2)}, u32[]{:S(2)}) collective-permute-start(bf16[16,1024]{1,0:T(8,128)(2,1)S(1)} %fusion), channel_id=1, source_target_pairs={{0,2},{2,0},{4,6},{6,4},{8,10},{10,8},{12,14},{14,12},{16,18},{18,... | collective-permute-start | bytes 98312 | tf_op jit(solution)/shard_map/ppermute | solution.py:436
  60.1 8.7 %collective-permute-start.8 = (bf16[16,1024]{1,0:T(8,128)(2,1)S(1)}, bf16[16,1024]{1,0:T(8,128)(2,1)S(1)}, u32[]{:S(2)}, u32[]{:S(2)}) collective-permute-start(bf16[16,1024]{1,0:T(8,128)(2,1)S(1)} %fusion.1), channel_id=1, source_target_pairs={{0,24},{2,26},{4,28},{6,30},{8,16},{10,18},{12,20},{14,22},{16,8},... | collective-permute-start | bytes 98312 | tf_op jit(solution)/shard_map/ppermute | solution.py:436
  61.7 7.1 %collective-permute-start.7 = (bf16[16,1024]{1,0:T(8,128)(2,1)S(1)}, bf16[16,1024]{1,0:T(8,128)(2,1)S(1)}, u32[]{:S(2)}, u32[]{:S(2)}) collective-permute-start(bf16[16,1024]{1,0:T(8,128)(2,1)S(1)} %fusion.1), channel_id=1, source_target_pairs={{0,16},{2,18},{4,20},{6,22},{8,24},{10,26},{12,28},{14,30},{16,0},... | collective-permute-start | bytes 98312 | tf_op jit(solution)/shard_map/ppermute | solution.py:436
  62.7 6.1 %collective-permute-start.6 = (bf16[16,1024]{1,0:T(8,128)(2,1)S(1)}, bf16[16,1024]{1,0:T(8,128)(2,1)S(1)}, u32[]{:S(2)}, u32[]{:S(2)}) collective-permute-start(bf16[16,1024]{1,0:T(8,128)(2,1)S(1)} %fusion.1), channel_id=1, source_target_pairs={{0,8},{2,10},{4,12},{6,14},{8,0},{10,2},{12,4},{14,6},{16,24},{18,... | collective-permute-start | bytes 98312 | tf_op jit(solution)/shard_map/ppermute | solution.py:436
